TPU v7x, 512 devices: a whole 4x8x8 slice. The times are simulated.
512 devices in a mesh: tm: 32 (over z, x), tile: 16 (over y, core).
Axes of the slice: x: 4, y: 8, z: 8, core: 2. Of those that a mesh axis runs over, the one named last changes fastest.
Arguments:
- features: bfloat16 [32, 32, 160, 512], P('tm', 'tile'), may hold values from -200 to 200, as said below
- norm_gain: float32 [512], replicated, may hold values from 0.1 to 1.9
- query_weight: bfloat16 [512, 512], replicated, may hold values from -7.9991455 to 7.9991455, as said below
- key_weight: bfloat16 [512, 512], replicated, may hold values from -0.25 to 0.25
- value_weight: bfloat16 [512, 512], replicated, may hold values from -0.25 to 0.25
- out_weight: bfloat16 [512, 512], replicated, may hold values from -0.5 to 0.5
- conv_weight: bfloat16 [3, 3, 3, 512, 256], replicated, may hold values from -0.0546875 to 0.0546875
- skip_weight: bfloat16 [512, 256], replicated, may hold values from -0.125 to 0.125
Outputs:
- decoded: bfloat16 [64, 32, 160, 256], P('tm', 'tile')
Inputs may be any that keep to these rules, and one draw needn't show every extreme that they name: Latent features whose magnitude varies from row to row and column to column. `query_weight`: A dense projection matrix.
All inputs are finite; a program needn't handle non-finite values.
Results may differ from a plain program's by a relative error of at most 0.012.
The roundings to bfloat16 on the way count: a program that leaves them out, or rounds other values in their place, can miss the bound.
Values may be sent and summed in bfloat16 or wider, within the bound.
A program may use at most 128 MiB of HBM per device.

v0:
```python
import jax
import jax.numpy as jnp
from jax import lax
from jax.sharding import PartitionSpec as P

GROUPS = 32


def shifted(array, axis, by):
    devices = lax.axis_size(axis)
    pairs = [(i, i + by) for i in range(devices) if 0 <= i + by < devices]
    return lax.ppermute(array, axis, pairs)


def padded_2(block, sides, width):
    for axis, dim in sides:
        count = lax.axis_size(axis)
        forward = [(i, i + 1) for i in range(count - 1)]
        backward = [(target, source) for source, target in forward]
        low = lax.ppermute(
            lax.slice_in_dim(block, block.shape[dim] - width, None, axis=dim), axis, forward
        )
        high = lax.ppermute(lax.slice_in_dim(block, 0, width, axis=dim), axis, backward)
        block = jnp.concatenate([low, block, high], axis=dim)
    return block


def per_device(
    features,
    norm_gain,
    query_weight,
    key_weight,
    value_weight,
    out_weight,
    conv_weight,
    skip_weight,
):
    frames, tile_rows, tile_cols, channels = features.shape
    cell_count = tile_rows * tile_cols
    group_width = channels // GROUPS
    grouped = features.astype(jnp.float32).reshape(frames, cell_count, GROUPS, group_width)
    total, squared = lax.psum(
        (jnp.sum(grouped, axis=(1, 3)), jnp.sum(grouped * grouped, axis=(1, 3))), "tile"
    )
    population = lax.axis_size("tile") * cell_count * group_width
    mean = (total / population)[:, None, :, None]
    var = (squared / population)[:, None, :, None] - mean * mean
    normed = ((grouped - mean) * lax.rsqrt(var + 1e-06)).reshape(
        frames, cell_count, channels
    ) * norm_gain
    normed = normed.astype(jnp.bfloat16)
    queries = jnp.einsum(
        "fnc,cd->fnd", normed, query_weight, preferred_element_type=jnp.float32
    ).astype(jnp.bfloat16)
    key_local = jnp.einsum(
        "fnc,cd->fnd", normed, key_weight, preferred_element_type=jnp.float32
    ).astype(jnp.bfloat16)
    value_local = jnp.einsum(
        "fnc,cd->fnd", normed, value_weight, preferred_element_type=jnp.float32
    ).astype(jnp.bfloat16)
    key_rows, value_rows = (
        lax.all_gather(key_local, "tile", axis=1, tiled=True),
        lax.all_gather(value_local, "tile", axis=1, tiled=True),
    )
    scores = jnp.einsum(
        "fqc,fkc->fqk", queries, key_rows, preferred_element_type=jnp.float32
    ) * channels ** (-0.5)
    peak = jnp.max(scores, axis=2, keepdims=True)
    unnormed = jnp.exp(scores - peak)
    denominator = jnp.sum(unnormed, axis=2, keepdims=True)
    weights = unnormed.astype(jnp.bfloat16)
    attended = (
        jnp.einsum("fqk,fkc->fqc", weights, value_rows, preferred_element_type=jnp.float32)
        / denominator
    ).astype(jnp.bfloat16)
    change = jnp.einsum("fqc,cd->fqd", attended, out_weight, preferred_element_type=jnp.float32)
    mid = (features.astype(jnp.float32).reshape(frames, cell_count, channels) + change).astype(
        jnp.bfloat16
    )
    act = (
        jax.nn.silu(mid.astype(jnp.float32))
        .astype(jnp.bfloat16)
        .reshape(frames, tile_rows, tile_cols, channels)
    )
    first_span = lax.axis_index("tm") == 0
    arrived = shifted(act, "tm", 1)
    arrived = jnp.where(first_span, act, arrived)
    stacked = jnp.concatenate([arrived, act], axis=0)
    rimmed = padded_2(stacked, (("tile", 1),), 1)
    padded = jnp.pad(rimmed, ((0, 0), (0, 0), (1, 1), (0, 0)))
    pieces = [
        padded[:, offset_y : offset_y + tile_rows, offset_x : offset_x + tile_cols, :]
        for offset_y in range(3)
        for offset_x in range(3)
    ]
    patches = jnp.concatenate(pieces, axis=-1).reshape(frames + 1, cell_count, 9 * channels)
    patch_before = patches[:-1]
    patch_now = patches[1:]
    taps = conv_weight.reshape(3, 9 * channels, conv_weight.shape[-1])
    skip = jnp.einsum("fnc,cd->fnd", mid, skip_weight, preferred_element_type=jnp.float32)
    first_tap = jnp.einsum("fnc,cd->fnd", patch_before, taps[0], preferred_element_type=jnp.float32)
    even = (
        first_tap
        + jnp.einsum("fnc,cd->fnd", patch_before, taps[1], preferred_element_type=jnp.float32)
        + jnp.einsum("fnc,cd->fnd", patch_now, taps[2], preferred_element_type=jnp.float32)
        + skip
    )
    odd = (
        first_tap
        + jnp.einsum("fnc,cd->fnd", patch_now, taps[1], preferred_element_type=jnp.float32)
        + jnp.einsum("fnc,cd->fnd", patch_now, taps[2], preferred_element_type=jnp.float32)
        + skip
    )
    decoded = jnp.stack([even, odd], axis=1).astype(jnp.bfloat16)
    return decoded.reshape(2 * frames, tile_rows, tile_cols, conv_weight.shape[-1])


def solution(mesh):
    in_specs = (P("tm", "tile", None, None), P(), P(), P(), P(), P(), P(), P())
    out_specs = P("tm", "tile", None, None)
    return jax.shard_map(
        per_device, mesh=mesh, in_specs=in_specs, out_specs=out_specs, check_vma=False
    )
```

profile of v0, /device:TPU:1, one launch (start us, length us, event | category | flops | bytes accessed | tf_op | source)
XLA Modules:
  0.0 176.1 jit_solution(7068608001065423834)
XLA Ops:
  6.5 0.0 copy-start
  6.5 0.0 all-gather.5.cloned.1.call-start
  6.5 1.1 convert_reduce_fusion
  7.7 0.1 reduce_sum.34
  7.8 0.1 reduce_sum.50
  7.8 0.1 reduce_sum.38
  8.0 0.1 reduce_sum.51
  8.1 29.8 %all-reduce.1 = (f32[1,32]{1,0:T(1,128)S(1)}, f32[1,32]{1,0:T(1,128)S(1)}) all-reduce(f32[1,32]{1,0:T(1,128)S(1)} %bitcast.67, f32[1,32]{1,0:T(1,128)S(1)} %bitcast.66), channel_id=1, replica_groups=mesh['tm'=32,'tile'=16] {'tile'}, use_global_device_ids=true, to_apply=%region_5.0 | all-reduce | flops 64 | bytes 512 | tf_op jit(solution)/shard_map/psum | solution.py:42
  37.9 0.1 mul.60
  37.9 0.1 mul.61
  38.0 0.1 sub.39
  38.1 0.1 sub.40
  38.2 1.1 fusion.33
  39.3 2.1 %convolution_convert_fusion.1 = bf16[320,512]{1,0:T(8,128)(2,1)} fusion(bf16[320,512]{1,0:T(8,128)(2,1)S(1)} %fusion.33, bf16[512,512]{1,0:T(8,128)(2,1)} %param.11), kind=kOutput, calls=%fused_computation.17 | convolution fusion | flops 167936000 | bytes 1179648 | tf_op jit(solution)/shard_map/fnc,cd->fnd/dot_general | solution.py:55
  41.4 0.0 all-gather.5.cloned.1.call-update
  41.4 0.0 all-gather.7.cloned.1.call-start
  41.4 2.1 %convolution_convert_fusion = bf16[320,512]{1,0:T(8,128)(2,1)} fusion(bf16[320,512]{1,0:T(8,128)(2,1)S(1)} %fusion.33, bf16[512,512]{1,0:T(8,128)(2,1)} %param.12), kind=kOutput, calls=%fused_computation.16 | convolution fusion | flops 167936000 | bytes 1179648 | tf_op jit(solution)/shard_map/fnc,cd->fnd/dot_general | solution.py:58
  43.5 0.0 all-gather.7.cloned.1.call-update
  43.6 43.5 %all-gather.5.cloned.1.call-done = bf16[5120,512]{1,0:T(8,128)(2,1)} async-done(((bf16[320,512]{1,0:T(8,128)(2,1)}), bf16[5120,512]{1,0:T(8,128)(2,1)}) %all-gather.5.cloned.1.call-update) | async-done | bytes 5242896 | tf_op jit(solution)/shard_map/all_gather | solution.py:62
  87.0 0.0 copy-done
  87.0 7.3 %fusion.41 = (f32[320]{0:T(512)S(1)}, f32[320,5120]{1,0:T(8,128)}) fusion(bf16[5120,512]{1,0:T(8,128)(2,1)} %all-gather.5.cloned.1.call-done, bf16[320,512]{1,0:T(8,128)(2,1)S(1)} %fusion.33, bf16[512,512]{1,0:T(8,128)(2,1)S(1)} %copy-done), kind=kOutput, calls=%fused_computation.70 | convolution fusion | flops 1848934144 | bytes 12649728 | tf_op jit(solution)/shard_map/fqc,fkc->fqk/dot_general | solution.py:65
  94.4 4.0 %fusion = f32[320]{0:T(512)S(1)} fusion(f32[320,5120]{1,0:T(8,128)} %get-tuple-element.17, f32[320]{0:T(512)S(1)} %get-tuple-element.16), kind=kLoop, calls=%fused_computation.2 | loop fusion | flops 3276480 | bytes 6556160 | tf_op jit(solution)/shard_map/reduce_sum | solution.py:70
  98.3 35.6 %all-gather.7.cloned.1.call-done = bf16[5120,512]{1,0:T(8,128)(2,1)} async-done(((bf16[320,512]{1,0:T(8,128)(2,1)}), bf16[5120,512]{1,0:T(8,128)(2,1)}) %all-gather.7.cloned.1.call-update) | async-done | bytes 5242896 | tf_op jit(solution)/shard_map/all_gather | solution.py:63
  133.9 0.0 copy-done.1
  134.0 6.6 %fusion.27 = (bf16[320,512]{1,0:T(8,128)(2,1)S(1)}, bf16[320,512]{1,0:T(8,128)(2,1)S(1)}) fusion(bf16[512,512]{1,0:T(8,128)(2,1)S(1)} %copy-done.3, bf16[5120,512]{1,0:T(8,128)(2,1)} %all-gather.7.cloned.1.call-done, f32[320,5120]{1,0:T(8,128)} %get-tuple-element.17, f32[320]{0:T(512)S(1)} %get-tuple-element.16, f32[320]{0:T(512)S(1)} %fusion, ...), kind=kOutput, calls=%fused_computation.39 | convolution fusion | flops 1850572800 | bytes 13306368 | tf_op jit(solution)/shard_map/fqc,cd->fqd/dot_general | solution.py:76
  140.6 3.1 %collective-permute-start = (bf16[1,2,160,512]{3,2,1,0:T(8,128)(2,1)S(1)}, bf16[1,2,160,512]{3,2,1,0:T(8,128)(2,1)S(1)}, u32[]{:S(2)}, u32[]{:S(2)}) collective-permute-start(bf16[1,2,160,512]{3,2,1,0:T(8,128)(2,1)S(1)} %bitcast.54), channel_id=1, source_target_pairs={{0,16},{16,32},{32,48},{48,64},{64,80},{80,96},{96,112},{112,128},... | collective-permute-start | bytes 983048 | tf_op jit(solution)/shard_map/ppermute | solution.py:12
  143.7 6.8 %collective-permute-done = bf16[1,2,160,512]{3,2,1,0:T(8,128)(2,1)S(1)} collective-permute-done((bf16[1,2,160,512]{3,2,1,0:T(8,128)(2,1)S(1)}, bf16[1,2,160,512]{3,2,1,0:T(8,128)(2,1)S(1)}, u32[]{:S(2)}, u32[]{:S(2)}) %collective-permute-start) | collective-permute-done | bytes 327712 | tf_op jit(solution)/shard_map/ppermute | solution.py:12
  150.5 0.1 fusion.34
  150.6 4.0 %collective-permute-start.1 = (bf16[2,1,160,512]{3,2,1,0:T(8,128)(2,1)S(1)}, bf16[2,1,160,512]{3,2,1,0:T(8,128)(2,1)S(1)}, u32[]{:S(2)}, u32[]{:S(2)}) collective-permute-start(bf16[2,1,160,512]{3,2,1,0:T(8,128)(2,1)S(1)} %get-tuple-element.14), channel_id=1, source_target_pairs={{0,1},{1,2},{2,3},{3,4},{4,5},{5,6},{6,7},{7,8},{8,9},{9,10},{10,1... | collective-permute-start | bytes 983048 | tf_op jit(solution)/shard_map/ppermute | solution.py:20
  154.6 0.0 copy-start.2
  154.7 2.1 %collective-permute-start.2 = (bf16[2,1,160,512]{3,2,1,0:T(8,128)(2,1)S(1)}, bf16[2,1,160,512]{3,2,1,0:T(8,128)(2,1)S(1)}, u32[]{:S(2)}, u32[]{:S(2)}) collective-permute-start(bf16[2,1,160,512]{3,2,1,0:T(8,128)(2,1)S(1)} %get-tuple-element.15), channel_id=1, source_target_pairs={{1,0},{2,1},{3,2},{4,3},{5,4},{6,5},{7,6},{8,7},{9,8},{10,9},{11,1... | collective-permute-start | bytes 983048 | tf_op jit(solution)/shard_map/ppermute | solution.py:23
  156.7 3.8 %fusion.39 = (bf16[1,3,3,512,256]{4,3,2,1,0:T(8,128)(2,1)S(1)}, bf16[1,3,3,512,256]{4,3,2,1,0:T(8,128)(2,1)S(1)}, bf16[1,3,3,512,256]{4,3,2,1,0:T(8,128)(2,1)S(1)}) fusion(bf16[3,3,3,512,256]{4,3,2,1,0:T(8,128)(2,1)} %param.14), kind=kLoop, calls=%fused_computation.68 | loop fusion | bytes 14155776 | tf_op jit(solution)/shard_map/slice | solution.py:104
  160.6 0.2 fusion.46
  160.8 0.0 collective-permute-done.1
  160.8 2.3 %collective-permute-done.2 = bf16[2,1,160,512]{3,2,1,0:T(8,128)(2,1)S(1)} collective-permute-done((bf16[2,1,160,512]{3,2,1,0:T(8,128)(2,1)S(1)}, bf16[2,1,160,512]{3,2,1,0:T(8,128)(2,1)S(1)}, u32[]{:S(2)}, u32[]{:S(2)}) %collective-permute-start.2) | collective-permute-done | bytes 327712 | tf_op jit(solution)/shard_map/ppermute | solution.py:23
  163.2 0.4 select_maximum_fusion
  163.5 0.1 slice_dynamic-update-slice_fusion.5
  163.7 0.2 slice_dynamic-update-slice_fusion.4
  163.8 0.1 slice_dynamic-update-slice_fusion.3
  163.9 0.2 slice_dynamic-update-slice_fusion.2
  164.1 0.1 slice_dynamic-update-slice_fusion.1
  164.2 0.2 slice_dynamic-update-slice_fusion
  164.4 0.4 fusion.40
  164.8 0.9 fusion.44
  165.7 0.9 fusion.45
  166.6 0.9 fusion.20
  167.6 0.9 fusion.21
  168.5 0.8 pad_maximum_fusion.5
  (10 shorter events, 0.2 us)
Async XLA Ops:
  6.5 80.5 %copy-start = (bf16[512,512]{1,0:T(8,128)(2,1)S(1)}, bf16[512,512]{1,0:T(8,128)(2,1)}, u32[]{:S(2)}) copy-start(bf16[512,512]{1,0:T(8,128)(2,1)} %param.10) | copy-start | bytes 1572868
  6.5 80.5 %all-gather.5.cloned.1.call-start = ((), (), s32[]{:S(2)}) async-start(), calls=%async_computation | async-start | bytes 5570560 | tf_op jit(solution)/shard_map/all_gather | solution.py:62
  41.4 92.6 %all-gather.7.cloned.1.call-start = ((), (), s32[]{:S(2)}) async-start(), calls=%async_computation.1 | async-start | bytes 5570560 | tf_op jit(solution)/shard_map/all_gather | solution.py:63
  94.4 39.6 %copy-start.1 = (bf16[1,2,160,512]{3,2,1,0:T(8,128)(2,1)S(1)}, bf16[1,2,160,512]{3,2,1,0:T(8,128)(2,1)}, u32[]{:S(2)}) copy-start(bf16[1,2,160,512]{3,2,1,0:T(8,128)(2,1)} %param.8) | copy-start | bytes 983044
  94.4 39.6 %copy-start.3 = (bf16[512,512]{1,0:T(8,128)(2,1)S(1)}, bf16[512,512]{1,0:T(8,128)(2,1)}, u32[]{:S(2)}) copy-start(bf16[512,512]{1,0:T(8,128)(2,1)} %param.13) | copy-start | bytes 1572868
  140.6 9.9 %collective-permute-start = (bf16[1,2,160,512]{3,2,1,0:T(8,128)(2,1)S(1)}, bf16[1,2,160,512]{3,2,1,0:T(8,128)(2,1)S(1)}, u32[]{:S(2)}, u32[]{:S(2)}) collective-permute-start(bf16[1,2,160,512]{3,2,1,0:T(8,128)(2,1)S(1)} %bitcast.54), channel_id=1, source_target_pairs={{0,16},{16,32},{32,48},{48,64},{64,80},{80,96},{96,112},{112,128},... | collective-permute-start | bytes 983048 | tf_op jit(solution)/shard_map/ppermute | solution.py:12
  150.6 10.2 %collective-permute-start.1 = (bf16[2,1,160,512]{3,2,1,0:T(8,128)(2,1)S(1)}, bf16[2,1,160,512]{3,2,1,0:T(8,128)(2,1)S(1)}, u32[]{:S(2)}, u32[]{:S(2)}) collective-permute-start(bf16[2,1,160,512]{3,2,1,0:T(8,128)(2,1)S(1)} %get-tuple-element.14), channel_id=1, source_target_pairs={{0,1},{1,2},{2,3},{3,4},{4,5},{5,6},{6,7},{7,8},{8,9},{9,10},{10,1... | collective-permute-start | bytes 983048 | tf_op jit(solution)/shard_map/ppermute | solution.py:20
  154.6 5.9 %copy-start.2 = (bf16[512,256]{1,0:T(8,128)(2,1)S(1)}, bf16[512,256]{1,0:T(8,128)(2,1)}, u32[]{:S(2)}) copy-start(bf16[512,256]{1,0:T(8,128)(2,1)} %param.15) | copy-start | bytes 786436
  154.7 8.5 %collective-permute-start.2 = (bf16[2,1,160,512]{3,2,1,0:T(8,128)(2,1)S(1)}, bf16[2,1,160,512]{3,2,1,0:T(8,128)(2,1)S(1)}, u32[]{:S(2)}, u32[]{:S(2)}) collective-permute-start(bf16[2,1,160,512]{3,2,1,0:T(8,128)(2,1)S(1)} %get-tuple-element.15), channel_id=1, source_target_pairs={{1,0},{2,1},{3,2},{4,3},{5,4},{6,5},{7,6},{8,7},{9,8},{10,9},{11,1... | collective-permute-start | bytes 983048 | tf_op jit(solution)/shard_map/ppermute | solution.py:23
Sparse Core Ops, SparseCore 0:
  41.5 45.4 all-gather.4
  89.1 44.7 all-gather.6
where the time goes:
time: 178 us; the launch traced here: 176 us
  waiting for transfers between devices  88.3 us (50%)
  blocking collectives  29.8 us (17%)
  matrix products  22.1 us (12%)
  between operations  13.6 us (8%)
  starting transfers between devices  9.25 us (5%)
  other arithmetic  7.78 us (4%)
  local copies, waits for them, and re-layouts  5.34 us (3%)
    all_gather x1, waiting for transfers between devices, per_device(): lax.all_gather(key_local, 'tile', axis=1, tiled=True)  43.5 us
    all_gather x1, waiting for transfers between devices, per_device(): lax.all_gather(value_local, 'tile', axis=1, tiled=True)  35.6 us
    psum x1, blocking collectives, per_device(): lax.psum((jnp.sum(grouped, axis=(1, 3)), jnp.sum(grouped * grouped, axis=...  29.8 us
    dot_general x1, matrix products, per_device(): jnp.einsum('fqc,fkc->fqk', queries, key_rows, preferred_element_type=jnp....  7.33 us
    ppermute x1, waiting for transfers between devices, shifted(): return lax.ppermute(array, axis, pairs)  6.79 us
    dot_general x1, matrix products, per_device(): jnp.einsum('fqc,cd->fqd', attended, out_weight, preferred_element_type=jn...  6.61 us
    ppermute x1, starting transfers between devices, padded_2(): lax.ppermute(lax.slice_in_dim(block, block.shape[dim] - width, None, axis...  4.04 us
    reduce_sum x1, other arithmetic, per_device(): denominator = jnp.sum(unnormed, axis=2, keepdims=True)  3.96 us
  transfers between devices with their start and end apart: 5, of which 4 were waited for; matrix products, arithmetic and copies ran while one was open for 10% of the time, Pallas kernels for 0%

commit v1 on v0

v1 whole, which is shorter than its diff:
```python
import functools
import math

import jax
import jax.numpy as jnp
from jax import lax
from jax.experimental import pallas as pl
from jax.experimental.pallas import tpu as pltpu
from jax.sharding import PartitionSpec as P

GROUPS = 32
EPS = 1e-06
MESH = pl.DeviceIdType.MESH
F32 = jnp.float32
BF16 = jnp.bfloat16


def group_sum(v, width):
    lanes = v.shape[-1]
    lane = lax.broadcasted_iota(jnp.int32, v.shape, 1)
    step = 1
    while step < width:
        above = pltpu.roll(v, lanes - step, 1)
        below = pltpu.roll(v, step, 1)
        v = v + jnp.where((lane & step) == 0, above, below)
        step *= 2
    return v


def kernel(
    spans, tiles, x_hbm, gain_ref, wq_hbm, wk_hbm, wv_hbm, wo_hbm, wc_hbm, ws_hbm,
    out_ref,
    slots, q2, acc, peak, total, stats, mid, act, even, odd, ab,
    wq, wk, wv, wo, wc, ws,
    ring_send, ring_recv, sib_send, sib_recv, st_send, st_recv, edge_send, edge_recv, load_sem, conv_sem,
):
    rows, cols, channels = x_hbm.shape
    cells = rows * cols
    out_channels = ws.shape[1]
    width = channels // GROUPS
    blocks = channels // 128
    chips = tiles // 2
    steps = chips

    t = lax.axis_index("tm")
    i = lax.axis_index("tile")
    y = i // 2
    core = i - 2 * y
    right = lax.rem(i + 2, tiles)
    left = lax.rem(i + tiles - 2, tiles)
    sibling = 2 * y + 1 - core
    above = lax.rem(i + tiles - 1, tiles)
    below = lax.rem(i + 1, tiles)
    t_next = lax.rem(t + 1, spans)
    t_prev = lax.rem(t + spans - 1, spans)

    def remote(src, dst, send, recv, where):
        return pltpu.make_async_remote_copy(
            src_ref=src, dst_ref=dst, send_sem=send, recv_sem=recv, device_id=where, device_id_type=MESH
        )

    loads = [
        pltpu.make_async_copy(x_hbm, slots.at[0, pl.ds(0, 2)], load_sem.at[0]),
        pltpu.make_async_copy(wq_hbm, wq, load_sem.at[1]),
        pltpu.make_async_copy(wk_hbm, wk, load_sem.at[2]),
        pltpu.make_async_copy(wv_hbm, wv, load_sem.at[3]),
        pltpu.make_async_copy(wo_hbm, wo, load_sem.at[4]),
        pltpu.make_async_copy(ws_hbm, ws, load_sem.at[5]),
    ]
    loads[0].start()

    barrier = pltpu.get_barrier_semaphore()

    def greet(k, carry):
        pl.semaphore_signal(barrier, inc=1, device_id=(t, lax.rem(i + k, tiles)), device_id_type=MESH)
        return carry

    lax.fori_loop(1, tiles, greet, 0)
    pl.semaphore_signal(barrier, inc=1, device_id=(t_next, i), device_id_type=MESH)
    pl.semaphore_signal(barrier, inc=1, device_id=(t_prev, i), device_id_type=MESH)
    pl.semaphore_wait(barrier, tiles + 1)

    def first(h, lane):
        row = h if lane == 0 else 1 - h
        return remote(
            x_hbm.at[row], slots.at[1 + h, lane], ring_send.at[1 + h, lane], ring_recv.at[1 + h, lane],
            (t, right if lane == 0 else left),
        )

    for h in range(2):
        for lane in range(2):
            first(h, lane).start()
    own_to_sibling = remote(
        x_hbm, slots.at[0, pl.ds(2, 2)], sib_send.at[0], sib_recv.at[0], (t, sibling)
    )
    own_to_sibling.start()

    for copy in loads[1:]:
        copy.start()

    def load_tap(k, carry):
        dt = k // 9
        dy = (k - 9 * dt) // 3
        dx = k - 9 * dt - 3 * dy
        column = pl.multiple_of(dt * out_channels, out_channels)
        pltpu.make_async_copy(
            wc_hbm.at[dt, dy, dx], wc.at[dx, dy, :, pl.ds(column, out_channels)], conv_sem.at[k]
        ).start()
        return carry

    lax.fori_loop(0, 27, load_tap, 0)

    loads[0].wait()
    own = slots[0, 0:2].reshape(cells, channels).astype(F32)
    sums = jnp.sum(own, axis=0, keepdims=True)
    squares = jnp.sum(own * own, axis=0, keepdims=True)
    sums = group_sum(jnp.broadcast_to(sums, (8, channels)), width)
    squares = group_sum(jnp.broadcast_to(squares, (8, channels)), width)
    lane_of = lax.broadcasted_iota(jnp.int32, (8, 128), 1) & (width - 1)
    packed = jnp.zeros((8, 128), F32)
    for k in range(2 * blocks):
        source = sums if k < blocks else squares
        b = k % blocks
        packed = jnp.where(lane_of == k, source[:, b * 128:(b + 1) * 128], packed)
    stats[0] = packed[0:1]

    def stat_copy(k):
        return remote(
            stats.at[0], stats.at[k], st_send.at[k], st_recv.at[k], (t, lax.rem(i + k, tiles))
        )

    def send_stat(k, carry):
        stat_copy(k).start()
        return carry

    lax.fori_loop(1, tiles, send_stat, 0)

    def ring_copy(e, lane):
        return remote(
            slots.at[e, lane], slots.at[e + 2, lane], ring_send.at[e + 2, lane], ring_recv.at[e + 2, lane],
            (t, right if lane == 0 else left),
        )

    def ring_arrival(e, lane):
        return remote(
            slots.at[e, lane], slots.at[e, lane], ring_send.at[e, lane], ring_recv.at[e, lane],
            (t, right if lane == 0 else left),
        )

    def sib_copy(e):
        return remote(
            slots.at[e, pl.ds(0, 2)], slots.at[e, pl.ds(2, 2)], sib_send.at[e], sib_recv.at[e], (t, sibling)
        )

    def prepare():
        def take(k, carry):
            stat_copy(k).wait_recv()
            return carry

        lax.fori_loop(1, tiles, take, 0)
        whole = stats[0]
        for k in range(1, tiles):
            whole = whole + stats[k]
        whole = jnp.broadcast_to(whole, (8, 128))
        spread = [group_sum(jnp.where(lane_of == k, whole, 0.0), width) for k in range(2 * blocks)]
        population = float(tiles * cells * width)
        mean = jnp.concatenate(spread[:blocks], axis=1)[0:1] / population
        var = jnp.concatenate(spread[blocks:], axis=1)[0:1] / population - mean * mean
        rstd = lax.rsqrt(var + EPS)
        gain = gain_ref[...]
        ab[0:1] = rstd * gain
        ab[1:2] = -mean * rstd * gain
        block = slots[0, 0:2].reshape(cells, channels).astype(F32)
        normed = (((block - mean) * rstd) * gain).astype(BF16)
        loads[1].wait()
        queries = jnp.dot(normed, wq[...], preferred_element_type=F32).astype(BF16)
        loads[2].wait()
        inner = lax.dot_general(queries, wk[...], (((1,), (1,)), ((), ())), preferred_element_type=F32)
        scale = channels ** (-0.5) * math.log2(math.e)
        q2[...] = (inner * (rstd * gain * scale)).astype(BF16)
        acc[...] = jnp.zeros_like(acc)
        total[...] = jnp.zeros_like(total)
        peak[...] = jnp.full_like(peak, -jnp.inf)

    def attend(e):
        keys = slots[e].reshape(4 * cols, channels)
        scores = lax.dot_general(q2[...], keys, (((1,), (1,)), ((), ())), preferred_element_type=F32)
        before = peak[:, 0:1]
        now = jnp.maximum(before, jnp.max(scores, axis=1, keepdims=True))
        fade = jnp.exp2(before - now)
        weights = jnp.exp2(scores - now).astype(BF16)
        peak[...] = jnp.broadcast_to(now, peak.shape)
        total[...] = total[...] * fade + jnp.sum(weights.astype(F32), axis=1, keepdims=True)
        acc[...] = acc[...] * fade + jnp.dot(weights, keys, preferred_element_type=F32)

    def gather_step(e, carry):
        @pl.when(e < steps - 1)
        def _():
            for lane in range(2):
                ring_arrival(e + 1, lane).wait_recv()

                @pl.when(e < steps - 3)
                def _():
                    ring_copy(e + 1, lane).start()

            sib_copy(e + 1).start()

        @pl.when(e == 0)
        def _():
            prepare()

        sib_copy(e).wait_recv()
        attend(e)
        return carry

    lax.fori_loop(0, steps, gather_step, 0)

    loads[3].wait()
    loads[4].wait()

    def halo_up(which):
        return remote(
            act.at[which, 1], act.at[which, 3], edge_send.at[2 * which], edge_recv.at[2 * which], (t, above)
        )

    def halo_down(which):
        return remote(
            act.at[which, 2], act.at[which, 0], edge_send.at[2 * which + 1], edge_recv.at[2 * which + 1], (t, below)
        )

    def onward(row):
        return remote(
            act.at[0, 1 + row], act.at[1, 1 + row], edge_send.at[4 + row], edge_recv.at[4 + row], (t_next, i)
        )

    def finish(k, carry):
        row = k + core - 2 * k * core
        part = pl.ds(pl.multiple_of(row * cols, cols), cols)
        mixed = acc[part, :] * (1.0 / total[part, 0:1])
        mixed = (mixed * ab[0:1] + ab[1:2]).astype(BF16)
        attended = jnp.dot(mixed, wv[...], preferred_element_type=F32).astype(BF16)
        change = jnp.dot(attended, wo[...], preferred_element_type=F32)
        mid_row = (slots[0, row].astype(F32) + change).astype(BF16)
        mid[part, :] = mid_row
        wide = mid_row.astype(F32)
        act[0, 1 + row] = (wide * (1.0 / (1.0 + jnp.exp(-wide)))).astype(BF16)
        onward(row).start()

        @pl.when(row == 0)
        def _():
            halo_up(0).start()

        @pl.when(row == 1)
        def _():
            halo_down(0).start()

        return carry

    lax.fori_loop(0, 2, finish, 0)

    loads[5].wait()

    def tap_wait(k, carry):
        dt = k // 9
        dy = (k - 9 * dt) // 3
        dx = k - 9 * dt - 3 * dy
        column = pl.multiple_of(dt * out_channels, out_channels)
        pltpu.make_async_copy(
            wc_hbm.at[dt, dy, dx], wc.at[dx, dy, :, pl.ds(column, out_channels)], conv_sem.at[k]
        ).wait()
        return carry

    lax.fori_loop(0, 27, tap_wait, 0)
    skip = jnp.dot(mid[...], ws[...], preferred_element_type=F32)
    even[...] = skip
    odd[...] = skip
    position = lax.rem(lax.broadcasted_iota(jnp.int32, (cells, 1), 0), cols)

    def product(which, dx, start):
        z = None
        for dy in range(3):
            piece = act[which, dy:dy + 2].reshape(cells, channels)
            part = jnp.dot(piece, wc[dx, dy, :, start:start + 2 * out_channels], preferred_element_type=F32)
            z = part if z is None else z + part
        if dx == 0:
            z = jnp.where(position == 0, 0.0, pltpu.roll(z, 1, 0))
        if dx == 2:
            z = jnp.where(position == cols - 1, 0.0, pltpu.roll(z, cells - 1, 0))
        return z[:, :out_channels], z[:, out_channels:]

    def clear(which):
        @pl.when(i == 0)
        def _():
            act[which, 0] = jnp.zeros((cols, channels), BF16)

        @pl.when(i == tiles - 1)
        def _():
            act[which, 3] = jnp.zeros((cols, channels), BF16)

    halo_up(0).wait_recv()
    halo_down(0).wait_recv()
    clear(0)
    for dx in range(3):
        second, third = product(0, dx, out_channels)
        even[...] += third
        odd[...] += second + third

    def pass_on(k, carry):
        row = k + core - 2 * k * core
        onward(row).wait_recv()

        @pl.when(row == 0)
        def _():
            halo_up(1).start()

        @pl.when(row == 1)
        def _():
            halo_down(1).start()

        return carry

    lax.fori_loop(0, 2, pass_on, 0)
    halo_up(1).wait_recv()
    halo_down(1).wait_recv()
    clear(1)
    which = jnp.where(t == 0, 0, 1)
    for dx in range(3):
        one, second = product(which, dx, 0)
        even[...] += one + second
        odd[...] += one
    out_ref[0] = even[...].astype(BF16)
    out_ref[1] = odd[...].astype(BF16)

    for h in range(2):
        for lane in range(2):
            first(h, lane).wait_send()
    own_to_sibling.wait_send()

    def drain(e, carry):
        for lane in range(2):
            @pl.when(e < steps - 2)
            def _():
                ring_copy(e, lane).wait_send()
        sib_copy(e).wait_send()
        return carry

    lax.fori_loop(1, steps, drain, 0)

    def drain_stat(k, carry):
        stat_copy(k).wait_send()
        return carry

    lax.fori_loop(1, tiles, drain_stat, 0)
    for which_act in range(2):
        halo_up(which_act).wait_send()
        halo_down(which_act).wait_send()
    for row in range(2):
        onward(row).wait_send()


def per_device(
    spans, tiles, features, norm_gain, query_weight, key_weight, value_weight, out_weight, conv_weight, skip_weight
):
    frames, rows, cols, channels = features.shape
    out_channels = conv_weight.shape[-1]
    cells = rows * cols
    steps = tiles // 2
    anywhere = pl.BlockSpec(memory_space=pl.ANY)
    vmem = pl.BlockSpec(memory_space=pltpu.VMEM)
    dma = pltpu.SemaphoreType.DMA
    out = pl.pallas_call(
        functools.partial(kernel, spans, tiles),
        out_shape=jax.ShapeDtypeStruct((2, cells, out_channels), BF16),
        in_specs=[anywhere, vmem] + [anywhere] * 6,
        out_specs=vmem,
        scratch_shapes=[
            pltpu.VMEM((steps, 4, cols, channels), BF16),
            pltpu.VMEM((cells, channels), BF16),
            pltpu.VMEM((cells, channels), F32),
            pltpu.VMEM((cells, 128), F32),
            pltpu.VMEM((cells, 128), F32),
            pltpu.VMEM((tiles, 1, 128), F32),
            pltpu.VMEM((cells, channels), BF16),
            pltpu.VMEM((2, 4, cols, channels), BF16),
            pltpu.VMEM((cells, out_channels), F32),
            pltpu.VMEM((cells, out_channels), F32),
            pltpu.VMEM((8, channels), F32),
            pltpu.VMEM((channels, channels), BF16),
            pltpu.VMEM((channels, channels), BF16),
            pltpu.VMEM((channels, channels), BF16),
            pltpu.VMEM((channels, channels), BF16),
            pltpu.VMEM((3, 3, channels, 3 * out_channels), BF16),
            pltpu.VMEM((channels, out_channels), BF16),
            dma((steps, 2)), dma((steps, 2)), dma((steps,)), dma((steps,)),
            dma((tiles,)), dma((tiles,)), dma((6,)), dma((6,)), dma((6,)), dma((27,)),
        ],
        compiler_params=pltpu.CompilerParams(
            collective_id=0, has_side_effects=True, vmem_limit_bytes=50 * 1024 * 1024
        ),
        name="mid_block_decode",
    )(
        features.reshape(rows, cols, channels), norm_gain.reshape(1, channels),
        query_weight, key_weight, value_weight, out_weight, conv_weight, skip_weight,
    )
    return out.reshape(2 * frames, rows, cols, out_channels)


def solution(mesh):
    spans, tiles = mesh.shape["tm"], mesh.shape["tile"]
    in_specs = (P("tm", "tile", None, None), P(), P(), P(), P(), P(), P(), P())
    return jax.shard_map(
        functools.partial(per_device, spans, tiles), mesh=mesh, in_specs=in_specs,
        out_specs=P("tm", "tile", None, None), check_vma=False,
    )
```

time: 178 us -> 71.5 us (0.40)
  waiting for transfers between devices: 88.3 us -> 0 us
  Pallas kernels: 0 us -> 63.6 us
  blocking collectives: 29.8 us -> 0 us
  matrix products: 22.1 us -> 0 us
  between operations: 13.6 us -> 0.02 us
  starting transfers between devices: 9.25 us -> 0 us
  other arithmetic: 7.78 us -> 0 us
  local copies, waits for them, and re-layouts: 5.34 us -> 7.49 us
    all_gather x2 -> x0, waiting for transfers between devices: 79.1 us -> none  [the longest x1 43.5 us: per_device(): lax.all_gather(key_local, 'tile', axis=1, tiled=True)]
    pallas_call x0 -> x1, Pallas kernels: none -> 63.6 us  [per_device(): pl.pallas_call(functools.partial(kernel, spans, tiles), out_shape=jax.Sha...]
    psum x1 -> x0, blocking collectives: 29.8 us -> none  [per_device(): lax.psum((jnp.sum(grouped, axis=(1, 3)), jnp.sum(grouped * grouped, axis=...]
    dot_general x9 -> x0, matrix products: 22.1 us -> none  [the longest x1 7.33 us: per_device(): jnp.einsum('fqc,fkc->fqk', queries, key_rows, preferred_element_type=jnp....]
    ppermute x3 -> x0, starting transfers between devices: 9.2 us -> none  [the longest x1 4.04 us: padded_2(): lax.ppermute(lax.slice_in_dim(block, block.shape[dim] - width, None, axis...]
    ppermute x3 -> x0, waiting for transfers between devices: 9.13 us -> none  [the longest x1 6.79 us: shifted(): return lax.ppermute(array, axis, pairs)]
    unnamed x13 -> x15, local copies, waits for them, and re-layouts: 0.5 us -> 7.49 us
    reduce_sum x4 -> x0, other arithmetic: 5.34 us -> none  [the longest x1 3.96 us: per_device(): denominator = jnp.sum(unnormed, axis=2, keepdims=True)]
  transfers between devices with their start and end apart: 5 -> 0, of which waited for: 4 -> 0; matrix products, arithmetic and copies ran while one was open for 10% -> 0% of each run, Pallas kernels for 0% -> 0%
where the time goes in v1:
time: 71.5 us; the launch traced here: 71.1 us
  Pallas kernels  63.6 us (89%)
  local copies, waits for them, and re-layouts  7.49 us (10%)
    pallas_call x1, Pallas kernels, per_device(): pl.pallas_call(functools.partial(kernel, spans, tiles), out_shape=jax.Sha...  63.6 us
    unnamed x15, local copies, waits for them, and re-layouts  7.49 us

profile of v1, /device:TPU:1, one launch (start us, length us, event | category | flops | bytes accessed | tf_op | source)
XLA Modules:
  0.0 71.1 jit_solution(4600631783107562977)
XLA Ops:
  0.0 0.0 copy-start
  0.0 1.0 %copy-done = bf16[512,512]{1,0:T(8,128)(2,1)S(1)} copy-done((bf16[512,512]{1,0:T(8,128)(2,1)S(1)}, bf16[512,512]{1,0:T(8,128)(2,1)}, u32[]{:S(2)}) %copy-start) | copy-done | bytes 524312
  1.0 0.0 copy-start.1
  1.0 1.0 %copy-done.1 = bf16[512,512]{1,0:T(8,128)(2,1)S(1)} copy-done((bf16[512,512]{1,0:T(8,128)(2,1)S(1)}, bf16[512,512]{1,0:T(8,128)(2,1)}, u32[]{:S(2)}) %copy-start.1) | copy-done | bytes 524312
  2.1 0.0 copy-start.2
  2.1 1.0 %copy-done.2 = bf16[512,512]{1,0:T(8,128)(2,1)S(1)} copy-done((bf16[512,512]{1,0:T(8,128)(2,1)S(1)}, bf16[512,512]{1,0:T(8,128)(2,1)}, u32[]{:S(2)}) %copy-start.2) | copy-done | bytes 524312
  3.1 0.0 copy-start.3
  3.1 1.0 %copy-done.3 = bf16[512,512]{1,0:T(8,128)(2,1)S(1)} copy-done((bf16[512,512]{1,0:T(8,128)(2,1)S(1)}, bf16[512,512]{1,0:T(8,128)(2,1)}, u32[]{:S(2)}) %copy-start.3) | copy-done | bytes 524312
  4.2 0.0 copy-start.4
  4.2 1.0 %copy-done.4 = bf16[1,2,160,512]{3,2,1,0:T(8,128)(2,1)S(1)} copy-done((bf16[1,2,160,512]{3,2,1,0:T(8,128)(2,1)S(1)}, bf16[1,2,160,512]{3,2,1,0:T(8,128)(2,1)}, u32[]{:S(2)}) %copy-start.4) | copy-done | bytes 327704
  5.1 0.0 copy-start.5
  5.1 0.9 %copy-done.5 = bf16[512,256]{1,0:T(8,128)(2,1)S(1)} copy-done((bf16[512,256]{1,0:T(8,128)(2,1)S(1)}, bf16[512,256]{1,0:T(8,128)(2,1)}, u32[]{:S(2)}) %copy-start.5) | copy-done | bytes 262168
  6.1 0.0 copy-start.6
  6.1 0.7 copy-done.6
  6.8 63.6 %mid_block_decode.1 = bf16[2,320,256]{2,1,0:T(8,128)(2,1)S(1)} custom-call(bf16[2,160,512]{2,1,0:T(8,128)(2,1)S(1)} %bitcast.4, f32[1,512]{1,0:T(1,128)S(1)} %bitcast.5, bf16[512,512]{1,0:T(8,128)(2,1)S(1)} %copy-done, bf16[512,512]{1,0:T(8,128)(2,1)S(1)} %copy-done.1, bf16[512,512]{1,0:T(8,128)(2,1)S(1)} %copy-done.2, bf16[512,512]{1,0:T(8,128)(2,1)S(1)} %copy-done.3, ...), custom_call_target="tpu_custom_call" | custom-call | tf_op jit(solution)/shard_map/mid_block_decode/pallas_call | solution.py:371
  70.4 0.7 %copy.10 = bf16[2,2,160,256]{3,2,1,0:T(8,128)(2,1)} copy(bf16[2,2,160,256]{3,2,1,0:T(8,128)(2,1)S(1)} %bitcast.3) | data formatting | bytes 655360
Async XLA Ops:
  0.0 1.0 %copy-start = (bf16[512,512]{1,0:T(8,128)(2,1)S(1)}, bf16[512,512]{1,0:T(8,128)(2,1)}, u32[]{:S(2)}) copy-start(bf16[512,512]{1,0:T(8,128)(2,1)} %wq_hbm.1) | copy-start | bytes 1572868
  1.0 1.0 %copy-start.1 = (bf16[512,512]{1,0:T(8,128)(2,1)S(1)}, bf16[512,512]{1,0:T(8,128)(2,1)}, u32[]{:S(2)}) copy-start(bf16[512,512]{1,0:T(8,128)(2,1)} %wk_hbm.1) | copy-start | bytes 1572868
  2.1 1.0 %copy-start.2 = (bf16[512,512]{1,0:T(8,128)(2,1)S(1)}, bf16[512,512]{1,0:T(8,128)(2,1)}, u32[]{:S(2)}) copy-start(bf16[512,512]{1,0:T(8,128)(2,1)} %wv_hbm.1) | copy-start | bytes 1572868
  3.1 1.0 %copy-start.3 = (bf16[512,512]{1,0:T(8,128)(2,1)S(1)}, bf16[512,512]{1,0:T(8,128)(2,1)}, u32[]{:S(2)}) copy-start(bf16[512,512]{1,0:T(8,128)(2,1)} %wo_hbm.1) | copy-start | bytes 1572868
  4.2 1.0 %copy-start.4 = (bf16[1,2,160,512]{3,2,1,0:T(8,128)(2,1)S(1)}, bf16[1,2,160,512]{3,2,1,0:T(8,128)(2,1)}, u32[]{:S(2)}) copy-start(bf16[1,2,160,512]{3,2,1,0:T(8,128)(2,1)} %param.8) | copy-start | bytes 983044
  5.1 0.9 %copy-start.5 = (bf16[512,256]{1,0:T(8,128)(2,1)S(1)}, bf16[512,256]{1,0:T(8,128)(2,1)}, u32[]{:S(2)}) copy-start(bf16[512,256]{1,0:T(8,128)(2,1)} %ws_hbm.1) | copy-start | bytes 786436
  6.1 0.7 copy-start.6

commit v2 on v1

--- a/solution.py
+++ b/solution.py
@@ -76,9 +76,18 @@
         return carry
 
     lax.fori_loop(1, tiles, greet, 0)
-    pl.semaphore_signal(barrier, inc=1, device_id=(t_next, i), device_id_type=MESH)
-    pl.semaphore_signal(barrier, inc=1, device_id=(t_prev, i), device_id_type=MESH)
-    pl.semaphore_wait(barrier, tiles + 1)
+    has_next = t < spans - 1
+    has_prev = t > 0
+
+    @pl.when(has_next)
+    def _():
+        pl.semaphore_signal(barrier, inc=1, device_id=(t_next, i), device_id_type=MESH)
+
+    @pl.when(has_prev)
+    def _():
+        pl.semaphore_signal(barrier, inc=1, device_id=(t_prev, i), device_id_type=MESH)
+
+    pl.semaphore_wait(barrier, tiles - 1 + jnp.where(has_next, 1, 0) + jnp.where(has_prev, 1, 0))
 
     def first(h, lane):
         row = h if lane == 0 else 1 - h
@@ -87,16 +96,12 @@
             (t, right if lane == 0 else left),
         )
 
-    for h in range(2):
-        for lane in range(2):
-            first(h, lane).start()
+    for lane in range(2):
+        first(0, lane).start()
     own_to_sibling = remote(
         x_hbm, slots.at[0, pl.ds(2, 2)], sib_send.at[0], sib_recv.at[0], (t, sibling)
     )
     own_to_sibling.start()
-
-    for copy in loads[1:]:
-        copy.start()
 
     def load_tap(k, carry):
         dt = k // 9
@@ -107,8 +112,6 @@
             wc_hbm.at[dt, dy, dx], wc.at[dx, dy, :, pl.ds(column, out_channels)], conv_sem.at[k]
         ).start()
         return carry
-
-    lax.fori_loop(0, 27, load_tap, 0)
 
     loads[0].wait()
     own = slots[0, 0:2].reshape(cells, channels).astype(F32)
@@ -134,6 +137,10 @@
         return carry
 
     lax.fori_loop(1, tiles, send_stat, 0)
+    for lane in range(2):
+        first(1, lane).start()
+    for copy in loads[1:]:
+        copy.start()
 
     def ring_copy(e, lane):
         return remote(
@@ -193,27 +200,42 @@
         total[...] = total[...] * fade + jnp.sum(weights.astype(F32), axis=1, keepdims=True)
         acc[...] = acc[...] * fade + jnp.dot(weights, keys, preferred_element_type=F32)
 
-    def gather_step(e, carry):
-        @pl.when(e < steps - 1)
-        def _():
-            for lane in range(2):
-                ring_arrival(e + 1, lane).wait_recv()
-
-                @pl.when(e < steps - 3)
-                def _():
-                    ring_copy(e + 1, lane).start()
-
-            sib_copy(e + 1).start()
-
-        @pl.when(e == 0)
-        def _():
-            prepare()
-
+    def arrive(e):
+        for lane in range(2):
+            ring_arrival(e, lane).wait_recv()
+
+            @pl.when(e < steps - 2)
+            def _():
+                ring_copy(e, lane).start()
+
+        sib_copy(e).start()
+
+    def attend_step(e, carry):
         sib_copy(e).wait_recv()
         attend(e)
         return carry
 
-    lax.fori_loop(0, steps, gather_step, 0)
+    def gather_step(e, carry):
+        @pl.when(e < steps)
+        def _():
+            arrive(e)
+
+        @pl.when(e == 2)
+        def _():
+            prepare()
+
+        @pl.when(e == 3)
+        def _():
+            lax.fori_loop(0, 27, load_tap, 0)
+
+        low = jnp.where(e == 3, 1, e - 1)
+        low = jnp.where(e == 2, 0, low)
+        high = jnp.where(e == 2, 1, e)
+        high = jnp.where(e == 1, low, high)
+        lax.fori_loop(low, high, attend_step, 0)
+        return carry
+
+    lax.fori_loop(1, steps + 1, gather_step, 0)
 
     loads[3].wait()
     loads[4].wait()
@@ -244,7 +266,10 @@
         mid[part, :] = mid_row
         wide = mid_row.astype(F32)
         act[0, 1 + row] = (wide * (1.0 / (1.0 + jnp.exp(-wide)))).astype(BF16)
-        onward(row).start()
+
+        @pl.when(has_next)
+        def _():
+            onward(row).start()
 
         @pl.when(row == 0)
         def _():
@@ -319,10 +344,13 @@
 
         return carry
 
-    lax.fori_loop(0, 2, pass_on, 0)
-    halo_up(1).wait_recv()
-    halo_down(1).wait_recv()
-    clear(1)
+    @pl.when(has_prev)
+    def _():
+        lax.fori_loop(0, 2, pass_on, 0)
+        halo_up(1).wait_recv()
+        halo_down(1).wait_recv()
+        clear(1)
+
     which = jnp.where(t == 0, 0, 1)
     for dx in range(3):
         one, second = product(which, dx, 0)
@@ -351,11 +379,18 @@
         return carry
 
     lax.fori_loop(1, tiles, drain_stat, 0)
-    for which_act in range(2):
-        halo_up(which_act).wait_send()
-        halo_down(which_act).wait_send()
-    for row in range(2):
-        onward(row).wait_send()
+    halo_up(0).wait_send()
+    halo_down(0).wait_send()
+
+    @pl.when(has_prev)
+    def _():
+        halo_up(1).wait_send()
+        halo_down(1).wait_send()
+
+    @pl.when(has_next)
+    def _():
+        for row in range(2):
+            onward(row).wait_send()
 
 
 def per_device(
@@ -395,7 +430,7 @@
             dma((tiles,)), dma((tiles,)), dma((6,)), dma((6,)), dma((6,)), dma((27,)),
         ],
         compiler_params=pltpu.CompilerParams(
-            collective_id=0, has_side_effects=True, vmem_limit_bytes=50 * 1024 * 1024
+            collective_id=0, has_side_effects=True, vmem_limit_bytes=62 * 1024 * 1024
         ),
         name="mid_block_decode",
     )(

time: 71.5 us -> 55 us (0.77)
  the two profiles are of different devices: /device:TPU:1 before, /device:TPU:384 now
where the time goes in v2:
time: 55 us; the launch traced here: 54.8 us
  Pallas kernels  53.1 us (97%)
  local copies, waits for them, and re-layouts  1.72 us (3%)
    pallas_call x1, Pallas kernels, per_device(): pl.pallas_call(functools.partial(kernel, spans, tiles), out_shape=jax.Sha...  53.1 us
    unnamed x1, local copies, waits for them, and re-layouts  1.72 us

profile of v2, /device:TPU:384, one launch (start us, length us, event | category | flops | bytes accessed | tf_op | source)
XLA Modules:
  0.0 54.8 jit_solution(17315683412561103537)
XLA Ops:
  0.0 53.1 %mid_block_decode.1 = bf16[2,320,256]{2,1,0:T(8,128)(2,1)} custom-call(bf16[2,160,512]{2,1,0:T(8,128)(2,1)} %bitcast.4, f32[1,512]{1,0:T(1,128)} %bitcast.5, bf16[512,512]{1,0:T(8,128)(2,1)} %wq_hbm.1, bf16[512,512]{1,0:T(8,128)(2,1)} %wk_hbm.1, bf16[512,512]{1,0:T(8,128)(2,1)} %wv_hbm.1, bf16[512,512]{1,0:T(8,128)(2,1)} %wo_hbm.1, ...), custom_call_target="tpu_custom_call" | custom-call | tf_op jit(solution)/shard_map/mid_block_decode/pallas_call | solution.py:406
  53.1 1.7 %copy.10 = bf16[2,2,160,256]{3,2,1,0:T(8,128)(2,1)} copy(bf16[2,2,160,256]{3,2,1,0:T(8,128)(2,1)} %bitcast.3) | data formatting | bytes 655360

commit v3 on v2

v3 whole, which is shorter than its diff:
```python
import functools
import math

import jax
import jax.numpy as jnp
from jax import lax
from jax.experimental import pallas as pl
from jax.experimental.pallas import tpu as pltpu
from jax.sharding import PartitionSpec as P

GROUPS = 32
EPS = 1e-06
MESH = pl.DeviceIdType.MESH
F32 = jnp.float32
BF16 = jnp.bfloat16


def group_sum(v, width):
    lanes = v.shape[-1]
    lane = lax.broadcasted_iota(jnp.int32, v.shape, 1)
    step = 1
    while step < width:
        above = pltpu.roll(v, lanes - step, 1)
        below = pltpu.roll(v, step, 1)
        v = v + jnp.where((lane & step) == 0, above, below)
        step *= 2
    return v


def remote(src, dst, send, recv, where):
    return pltpu.make_async_remote_copy(
        src_ref=src, dst_ref=dst, send_sem=send, recv_sem=recv, device_id=where, device_id_type=MESH
    )


def kernel(
    spans, tiles, x_hbm, gain_hbm, wq_hbm, wk_hbm, wv_hbm, wo_hbm, wc_hbm, ws_hbm, out_ref,
    slots, q2, acc, peak, total, stats, ab, gain, wq, wk, wv, wo, ws,
    act, mid, near, far, base, wc,
    ring_send, ring_recv, sib_send, sib_recv, st_send, st_recv, load_sem, edge_send, edge_recv, conv_sem,
):
    rows, cols, channels = x_hbm.shape
    outs = ws.shape[1]
    cells = rows * cols
    width = channels // GROUPS
    blocks = channels // 128
    steps = tiles // 2

    t = lax.axis_index("tm")
    i = lax.axis_index("tile")
    y = i // 2
    core = i - 2 * y
    right = lax.rem(i + 2, tiles)
    left = lax.rem(i + tiles - 2, tiles)
    sibling = 2 * y + 1 - core
    above = lax.rem(i + tiles - 1, tiles)
    below = lax.rem(i + 1, tiles)
    t_next = lax.rem(t + 1, spans)
    t_prev = lax.rem(t + spans - 1, spans)
    has_next = t < spans - 1
    has_prev = t > 0

    loads = [
        pltpu.make_async_copy(x_hbm, slots.at[0, pl.ds(0, 2)], load_sem.at[0]),
        pltpu.make_async_copy(wq_hbm, wq, load_sem.at[1]),
        pltpu.make_async_copy(wk_hbm, wk, load_sem.at[2]),
        pltpu.make_async_copy(gain_hbm, gain, load_sem.at[3]),
        pltpu.make_async_copy(wv_hbm, wv, load_sem.at[4]),
        pltpu.make_async_copy(wo_hbm, wo, load_sem.at[5]),
        pltpu.make_async_copy(ws_hbm, ws, load_sem.at[6]),
    ]
    loads[0].start()

    barrier = pltpu.get_barrier_semaphore()

    def greet(k, carry):
        pl.semaphore_signal(barrier, inc=1, device_id=(t, lax.rem(i + k, tiles)), device_id_type=MESH)
        return carry

    lax.fori_loop(1, tiles, greet, 0)

    @pl.when(has_prev)
    def _():
        pl.semaphore_signal(barrier, inc=1, device_id=(t_prev, i), device_id_type=MESH)

    pl.semaphore_wait(barrier, tiles - 1 + jnp.where(has_next, 1, 0))

    def first(h, lane):
        row = h if lane == 0 else 1 - h
        return remote(
            x_hbm.at[row], slots.at[1 + h, lane], ring_send.at[1 + h, lane], ring_recv.at[1 + h, lane],
            (t, right if lane == 0 else left),
        )

    for lane in range(2):
        first(0, lane).start()
    own_to_sibling = remote(
        x_hbm, slots.at[0, pl.ds(2, 2)], sib_send.at[0], sib_recv.at[0], (t, sibling)
    )
    own_to_sibling.start()

    loads[0].wait()
    own = slots[0, 0:2].reshape(cells, channels).astype(F32)
    sums = jnp.sum(own, axis=0, keepdims=True)
    squares = jnp.sum(own * own, axis=0, keepdims=True)
    sums = group_sum(jnp.broadcast_to(sums, (8, channels)), width)
    squares = group_sum(jnp.broadcast_to(squares, (8, channels)), width)
    lane_of = lax.broadcasted_iota(jnp.int32, (8, 128), 1) & (width - 1)
    packed = jnp.zeros((8, 128), F32)
    for k in range(2 * blocks):
        source = sums if k < blocks else squares
        b = k % blocks
        packed = jnp.where(lane_of == k, source[:, b * 128:(b + 1) * 128], packed)
    stats[0] = packed[0:1]

    def stat_copy(k):
        return remote(
            stats.at[0], stats.at[k], st_send.at[k], st_recv.at[k], (t, lax.rem(i + k, tiles))
        )

    def send_stat(k, carry):
        stat_copy(k).start()
        return carry

    lax.fori_loop(1, tiles, send_stat, 0)
    for lane in range(2):
        first(1, lane).start()
    for copy in loads[1:]:
        copy.start()

    def ring_copy(e, lane):
        return remote(
            slots.at[e, lane], slots.at[e + 2, lane], ring_send.at[e + 2, lane], ring_recv.at[e + 2, lane],
            (t, right if lane == 0 else left),
        )

    def ring_arrival(e, lane):
        return remote(
            slots.at[e, lane], slots.at[e, lane], ring_send.at[e, lane], ring_recv.at[e, lane],
            (t, right if lane == 0 else left),
        )

    def sib_copy(e):
        return remote(
            slots.at[e, pl.ds(0, 2)], slots.at[e, pl.ds(2, 2)], sib_send.at[e], sib_recv.at[e], (t, sibling)
        )

    def prepare():
        def take(k, carry):
            stat_copy(k).wait_recv()
            return carry

        lax.fori_loop(1, tiles, take, 0)
        whole = stats[0]
        for k in range(1, tiles):
            whole = whole + stats[k]
        whole = jnp.broadcast_to(whole, (8, 128))
        spread = [group_sum(jnp.where(lane_of == k, whole, 0.0), width) for k in range(2 * blocks)]
        population = float(tiles * cells * width)
        mean = jnp.concatenate(spread[:blocks], axis=1)[0:1] / population
        var = jnp.concatenate(spread[blocks:], axis=1)[0:1] / population - mean * mean
        rstd = lax.rsqrt(var + EPS)
        loads[3].wait()
        scaled = rstd * gain[...]
        ab[0:1] = scaled
        ab[1:2] = -mean * scaled
        block = slots[0, 0:2].reshape(cells, channels).astype(F32)
        normed = (((block - mean) * rstd) * gain[...]).astype(BF16)
        loads[1].wait()
        queries = jnp.dot(normed, wq[...], preferred_element_type=F32).astype(BF16)
        loads[2].wait()
        inner = lax.dot_general(queries, wk[...], (((1,), (1,)), ((), ())), preferred_element_type=F32)
        scale = channels ** (-0.5) * math.log2(math.e)
        q2[...] = (inner * (scaled * scale)).astype(BF16)
        acc[...] = jnp.zeros_like(acc)
        total[...] = jnp.zeros_like(total)
        peak[...] = jnp.full_like(peak, -jnp.inf)

    def attend(e):
        keys = slots[e].reshape(4 * cols, channels)
        scores = lax.dot_general(q2[...], keys, (((1,), (1,)), ((), ())), preferred_element_type=F32)
        before = peak[:, 0:1]
        now = jnp.maximum(before, jnp.max(scores, axis=1, keepdims=True))
        fade = jnp.exp2(before - now)
        weights = jnp.exp2(scores - now).astype(BF16)
        peak[...] = jnp.broadcast_to(now, peak.shape)
        total[...] = total[...] * fade + jnp.sum(weights.astype(F32), axis=1, keepdims=True)
        acc[...] = acc[...] * fade + jnp.dot(weights, keys, preferred_element_type=F32)

    def arrive(e):
        for lane in range(2):
            ring_arrival(e, lane).wait_recv()

            @pl.when(e < steps - 2)
            def _():
                ring_copy(e, lane).start()

        sib_copy(e).start()

    def attend_step(e, carry):
        sib_copy(e).wait_recv()
        attend(e)
        return carry

    def tap(k):
        dt = k // 9
        dy = (k - 9 * dt) // 3
        dx = k - 9 * dt - 3 * dy
        column = pl.multiple_of(dt * outs, outs)
        return pltpu.make_async_copy(wc_hbm.at[dt, dy, dx], wc.at[dx, dy, :, pl.ds(column, outs)], conv_sem.at[k])

    def load_tap(k, carry):
        tap(k).start()
        return carry

    def take_tap(k, carry):
        tap(k).wait()
        return carry

    def gather_step(e, carry):
        @pl.when(e < steps)
        def _():
            arrive(e)

        @pl.when(e == 2)
        def _():
            prepare()

        @pl.when(e == 3)
        def _():
            lax.fori_loop(0, 27, load_tap, 0)

        low = jnp.where(e == 3, 1, e - 1)
        low = jnp.where(e == 2, 0, low)
        high = jnp.where(e == 2, 1, e)
        high = jnp.where(e == 1, low, high)
        lax.fori_loop(low, high, attend_step, 0)
        return carry

    lax.fori_loop(1, steps + 1, gather_step, 0)

    def halo_up(which):
        return remote(
            act.at[which, 1], act.at[which, 3], edge_send.at[2 * which], edge_recv.at[2 * which], (t, above)
        )

    def halo_down(which):
        return remote(
            act.at[which, 2], act.at[which, 0], edge_send.at[2 * which + 1], edge_recv.at[2 * which + 1], (t, below)
        )

    def onward(row):
        return remote(
            act.at[0, 1 + row], act.at[1, 1 + row], edge_send.at[4 + row], edge_recv.at[4 + row], (t_next, i)
        )

    def send_halo(which, row):
        @pl.when(row == 0)
        def _():
            halo_up(which).start()

        @pl.when(row == 1)
        def _():
            halo_down(which).start()

    loads[4].wait()
    loads[5].wait()

    def finish(k, carry):
        row = k + core - 2 * k * core
        part = pl.ds(pl.multiple_of(row * cols, cols), cols)
        mixed = (acc[part, :] * (1.0 / total[part, 0:1]) * ab[0:1] + ab[1:2]).astype(BF16)
        attended = jnp.dot(mixed, wv[...], preferred_element_type=F32).astype(BF16)
        change = jnp.dot(attended, wo[...], preferred_element_type=F32)
        mid_row = (slots[0, row].astype(F32) + change).astype(BF16)
        mid[part, :] = mid_row
        wide = mid_row.astype(F32)
        act[0, 1 + row] = (wide * (1.0 / (1.0 + jnp.exp(-wide)))).astype(BF16)

        @pl.when(has_next)
        def _():
            onward(row).start()

        send_halo(0, row)
        return carry

    lax.fori_loop(0, 2, finish, 0)

    loads[6].wait()
    skip = jnp.dot(mid[...], ws[...], preferred_element_type=F32)
    base[:, :outs] = skip
    base[:, outs:] = skip
    near[...] = jnp.zeros_like(near)
    far[...] = jnp.zeros_like(far)
    lax.fori_loop(0, 27, take_tap, 0)

    def visit(n):
        own = n < 4
        first = lax.rem(n, 2) == 0
        inner = n // 2
        mine = jnp.where(inner == 0, 1 + core, 2 - core)
        halo = jnp.where(first, 3 * core, 3 - 3 * core)
        source = jnp.where(own, mine, halo)
        same = jnp.where(inner == 0, core, 1 - core)
        target = jnp.where(own, jnp.where(first, same, 1 - same), jnp.where(first, core, 1 - core))
        return source, target, source - target

    def add_row(sums, which, n, start):
        source, target, dy = visit(n)
        row = act[which, source]
        part = pl.ds(pl.multiple_of(target * cols, cols), cols)
        for dx in range(3):
            sums[dx, part, :] += jnp.dot(row, wc[dx, dy, :, start:start + 2 * outs], preferred_element_type=F32)

    position = lax.rem(lax.broadcasted_iota(jnp.int32, (cells, 1), 0), cols)

    def shifted(z, dx):
        if dx == 0:
            return jnp.where(position == 0, 0.0, pltpu.roll(z, 1, 0))
        if dx == 2:
            return jnp.where(position == cols - 1, 0.0, pltpu.roll(z, cells - 1, 0))
        return z

    at_rim = jnp.where(core == 0, i == 0, i == tiles - 1)

    def near_step(n, carry):
        @pl.when(n == 4)
        def _():
            halo_up(0).wait_recv()
            halo_down(0).wait_recv()

        @pl.when(jnp.logical_not(jnp.logical_and(n == 4, at_rim)))
        def _():
            add_row(near, 0, n, outs)

        return carry

    lax.fori_loop(0, 6, near_step, 0)
    for dx in range(3):
        z = shifted(near[dx], dx)
        base[:, :outs] += z[:, outs:]
        base[:, outs:] += z[:, :outs] + z[:, outs:]

    which = jnp.where(t == 0, 0, 1)

    def far_step(n, carry):
        @pl.when(jnp.logical_and(has_prev, jnp.logical_or(n == 0, n == 2)))
        def _():
            row = jnp.where(n == 0, core, 1 - core)
            onward(row).wait_recv()
            send_halo(1, row)

        @pl.when(jnp.logical_and(has_prev, n == 4))
        def _():
            @pl.when(core == 0)
            def _():
                halo_down(1).wait_recv()

            @pl.when(core == 1)
            def _():
                halo_up(1).wait_recv()

        @pl.when(jnp.logical_and(has_prev, n == 5))
        def _():
            @pl.when(core == 0)
            def _():
                halo_up(1).wait_recv()

            @pl.when(core == 1)
            def _():
                halo_down(1).wait_recv()

        @pl.when(jnp.logical_not(jnp.logical_and(n == 4, at_rim)))
        def _():
            add_row(far, which, n, 0)

        return carry

    lax.fori_loop(0, 6, far_step, 0)
    even = base[:, :outs]
    odd = base[:, outs:]
    for dx in range(3):
        z = shifted(far[dx], dx)
        even = even + (z[:, :outs] + z[:, outs:])
        odd = odd + z[:, :outs]
    out_ref[0] = even.astype(BF16)
    out_ref[1] = odd.astype(BF16)

    for h in range(2):
        for lane in range(2):
            first(h, lane).wait_send()
    own_to_sibling.wait_send()

    def drain(e, carry):
        for lane in range(2):
            @pl.when(e < steps - 2)
            def _():
                ring_copy(e, lane).wait_send()
        sib_copy(e).wait_send()
        return carry

    lax.fori_loop(1, steps, drain, 0)

    def drain_stat(k, carry):
        stat_copy(k).wait_send()
        return carry

    lax.fori_loop(1, tiles, drain_stat, 0)
    halo_up(0).wait_send()
    halo_down(0).wait_send()

    @pl.when(has_prev)
    def _():
        halo_up(1).wait_send()
        halo_down(1).wait_send()

    @pl.when(has_next)
    def _():
        for row in range(2):
            onward(row).wait_send()


def per_device(
    spans, tiles, features, norm_gain, query_weight, key_weight, value_weight, out_weight, conv_weight, skip_weight
):
    frames, rows, cols, channels = features.shape
    outs = conv_weight.shape[-1]
    cells = rows * cols
    steps = tiles // 2
    hbm = pl.BlockSpec(memory_space=pltpu.HBM)
    dma = pltpu.SemaphoreType.DMA
    operands = (
        features.reshape(rows, cols, channels), norm_gain.reshape(1, channels),
        query_weight, key_weight, value_weight, out_weight, conv_weight, skip_weight,
    )
    operands = [pltpu.with_memory_space_constraint(operand, pltpu.HBM) for operand in operands]
    out = pl.pallas_call(
        functools.partial(kernel, spans, tiles),
        out_shape=jax.ShapeDtypeStruct((2, cells, outs), BF16),
        in_specs=[hbm] * 8,
        out_specs=pl.BlockSpec(memory_space=pltpu.VMEM),
        scratch_shapes=[
            pltpu.VMEM((steps, 4, cols, channels), BF16),
            pltpu.VMEM((cells, channels), BF16),
            pltpu.VMEM((cells, channels), F32),
            pltpu.VMEM((cells, 128), F32),
            pltpu.VMEM((cells, 128), F32),
            pltpu.VMEM((tiles, 1, 128), F32),
            pltpu.VMEM((8, channels), F32),
            pltpu.VMEM((1, channels), F32),
            pltpu.VMEM((channels, channels), BF16),
            pltpu.VMEM((channels, channels), BF16),
            pltpu.VMEM((channels, channels), BF16),
            pltpu.VMEM((channels, channels), BF16),
            pltpu.VMEM((channels, outs), BF16),
            pltpu.VMEM((2, 4, cols, channels), BF16),
            pltpu.VMEM((cells, channels), BF16),
            pltpu.VMEM((3, cells, 2 * outs), F32),
            pltpu.VMEM((3, cells, 2 * outs), F32),
            pltpu.VMEM((cells, 2 * outs), F32),
            pltpu.VMEM((3, 3, channels, 3 * outs), BF16),
            dma((steps, 2)), dma((steps, 2)), dma((steps,)), dma((steps,)), dma((tiles,)), dma((tiles,)), dma((7,)),
            dma((6,)), dma((6,)), dma((27,)),
        ],
        compiler_params=pltpu.CompilerParams(
            collective_id=0, has_side_effects=True, vmem_limit_bytes=50 * 1024 * 1024
        ),
        name="mid_block_decode",
    )(*operands)
    return out.reshape(2 * frames, rows, cols, outs)


def solution(mesh):
    spans, tiles = mesh.shape["tm"], mesh.shape["tile"]
    in_specs = (P("tm", "tile", None, None), P(), P(), P(), P(), P(), P(), P())
    return jax.shard_map(
        functools.partial(per_device, spans, tiles), mesh=mesh, in_specs=in_specs,
        out_specs=P("tm", "tile", None, None), check_vma=False,
    )
```

time: 55 us -> 52.1 us (0.947)
  the two profiles are of different devices: /device:TPU:384 before, /device:TPU:321 now
where the time goes in v3:
time: 52.1 us; the launch traced here: 51.9 us
  Pallas kernels  51.2 us (98%)
  local copies, waits for them, and re-layouts  0.73 us (1%)
    pallas_call x1, Pallas kernels, per_device(): pl.pallas_call(functools.partial(kernel, spans, tiles), out_shape=jax.Sha...  51.2 us

profile of v3, /device:TPU:321, one launch (start us, length us, event | category | flops | bytes accessed | tf_op | source)
XLA Modules:
  0.0 51.9 jit_solution(1905170547286420489)
XLA Ops:
  0.0 51.2 %mid_block_decode.1 = bf16[2,320,256]{2,1,0:T(8,128)(2,1)S(1)} custom-call(bf16[2,160,512]{2,1,0:T(8,128)(2,1)} %bitcast.4, f32[1,512]{1,0:T(1,128)} %bitcast.5, bf16[512,512]{1,0:T(8,128)(2,1)} %wq_hbm.1, bf16[512,512]{1,0:T(8,128)(2,1)} %wk_hbm.1, bf16[512,512]{1,0:T(8,128)(2,1)} %wv_hbm.1, bf16[512,512]{1,0:T(8,128)(2,1)} %wo_hbm.1, ...), custom_call_target="tpu_custom_call" | custom-call | tf_op jit(solution)/shard_map/mid_block_decode/pallas_call | solution.py:437
  51.2 0.7 %copy.10 = bf16[2,2,160,256]{3,2,1,0:T(8,128)(2,1)} copy(bf16[2,2,160,256]{3,2,1,0:T(8,128)(2,1)S(1)} %bitcast.3) | data formatting | bytes 655360

commit v4 on v3

--- a/solution.py
+++ b/solution.py
@@ -35,7 +35,7 @@
 
 def kernel(
     spans, tiles, x_hbm, gain_hbm, wq_hbm, wk_hbm, wv_hbm, wo_hbm, wc_hbm, ws_hbm, out_ref,
-    slots, q2, acc, peak, total, stats, ab, gain, wq, wk, wv, wo, ws,
+    slots, q2, acc, peak, total, stats, ab, gain, wq, wk, wv, wo, wvo, ws,
     act, mid, near, far, base, wc,
     ring_send, ring_recv, sib_send, sib_recv, st_send, st_recv, load_sem, edge_send, edge_recv, conv_sem,
 ):
@@ -83,23 +83,23 @@
     def _():
         pl.semaphore_signal(barrier, inc=1, device_id=(t_prev, i), device_id_type=MESH)
 
+    loads[0].wait()
     pl.semaphore_wait(barrier, tiles - 1 + jnp.where(has_next, 1, 0))
 
     def first(h, lane):
         row = h if lane == 0 else 1 - h
         return remote(
-            x_hbm.at[row], slots.at[1 + h, lane], ring_send.at[1 + h, lane], ring_recv.at[1 + h, lane],
+            slots.at[0, row], slots.at[1 + h, lane], ring_send.at[1 + h, lane], ring_recv.at[1 + h, lane],
             (t, right if lane == 0 else left),
         )
 
     for lane in range(2):
         first(0, lane).start()
     own_to_sibling = remote(
-        x_hbm, slots.at[0, pl.ds(2, 2)], sib_send.at[0], sib_recv.at[0], (t, sibling)
+        slots.at[0, pl.ds(0, 2)], slots.at[0, pl.ds(2, 2)], sib_send.at[0], sib_recv.at[0], (t, sibling)
     )
     own_to_sibling.start()
 
-    loads[0].wait()
     own = slots[0, 0:2].reshape(cells, channels).astype(F32)
     sums = jnp.sum(own, axis=0, keepdims=True)
     squares = jnp.sum(own * own, axis=0, keepdims=True)
@@ -176,8 +176,8 @@
         total[...] = jnp.zeros_like(total)
         peak[...] = jnp.full_like(peak, -jnp.inf)
 
-    def attend(e):
-        keys = slots[e].reshape(4 * cols, channels)
+    def attend(e, begin, count):
+        keys = slots[e, begin:begin + count].reshape(count * cols, channels)
         scores = lax.dot_general(q2[...], keys, (((1,), (1,)), ((), ())), preferred_element_type=F32)
         before = peak[:, 0:1]
         now = jnp.maximum(before, jnp.max(scores, axis=1, keepdims=True))
@@ -199,7 +199,7 @@
 
     def attend_step(e, carry):
         sib_copy(e).wait_recv()
-        attend(e)
+        attend(e, 0, 4)
         return carry
 
     def tap(k):
@@ -217,10 +217,23 @@
         tap(k).wait()
         return carry
 
+    def tap(k):
+        dt = k // 9
+        dy = (k - 9 * dt) // 3
+        dx = k - 9 * dt - 3 * dy
+        column = pl.multiple_of(dt * outs, outs)
+        return pltpu.make_async_copy(wc_hbm.at[dt, dy, dx], wc.at[dx, dy, :, pl.ds(column, outs)], conv_sem.at[k])
+
+    def load_tap(k, carry):
+        tap(k).start()
+        return carry
+
+    def take_tap(k, carry):
+        tap(k).wait()
+        return carry
+
     def gather_step(e, carry):
-        @pl.when(e < steps)
-        def _():
-            arrive(e)
+        arrive(e)
 
         @pl.when(e == 2)
         def _():
@@ -229,15 +242,23 @@
         @pl.when(e == 3)
         def _():
             lax.fori_loop(0, 27, load_tap, 0)
+            loads[4].wait()
+            loads[5].wait()
+            wvo[...] = jnp.dot(wv[...], wo[...], preferred_element_type=F32).astype(BF16)
 
         low = jnp.where(e == 3, 1, e - 1)
         low = jnp.where(e == 2, 0, low)
         high = jnp.where(e == 2, 1, e)
+        high = jnp.where(e == steps - 2, steps - 1, high)
         high = jnp.where(e == 1, low, high)
+        low = jnp.where(e == steps - 1, high, low)
         lax.fori_loop(low, high, attend_step, 0)
         return carry
 
-    lax.fori_loop(1, steps + 1, gather_step, 0)
+    lax.fori_loop(1, steps, gather_step, 0)
+    attend(steps - 1, 0, 2)
+    sib_copy(steps - 1).wait_recv()
+    attend(steps - 1, 2, 2)
 
     def halo_up(which):
         return remote(
@@ -262,16 +283,12 @@
         @pl.when(row == 1)
         def _():
             halo_down(which).start()
-
-    loads[4].wait()
-    loads[5].wait()
 
     def finish(k, carry):
         row = k + core - 2 * k * core
         part = pl.ds(pl.multiple_of(row * cols, cols), cols)
         mixed = (acc[part, :] * (1.0 / total[part, 0:1]) * ab[0:1] + ab[1:2]).astype(BF16)
-        attended = jnp.dot(mixed, wv[...], preferred_element_type=F32).astype(BF16)
-        change = jnp.dot(attended, wo[...], preferred_element_type=F32)
+        change = jnp.dot(mixed, wvo[...], preferred_element_type=F32)
         mid_row = (slots[0, row].astype(F32) + change).astype(BF16)
         mid[part, :] = mid_row
         wide = mid_row.astype(F32)
@@ -336,55 +353,64 @@
         return carry
 
     lax.fori_loop(0, 6, near_step, 0)
-    for dx in range(3):
-        z = shifted(near[dx], dx)
-        base[:, :outs] += z[:, outs:]
-        base[:, outs:] += z[:, :outs] + z[:, outs:]
-
     which = jnp.where(t == 0, 0, 1)
 
     def far_step(n, carry):
-        @pl.when(jnp.logical_and(has_prev, jnp.logical_or(n == 0, n == 2)))
+        @pl.when(jnp.logical_and(has_prev, lax.rem(n, 2) == 0))
         def _():
             row = jnp.where(n == 0, core, 1 - core)
             onward(row).wait_recv()
             send_halo(1, row)
 
-        @pl.when(jnp.logical_and(has_prev, n == 4))
-        def _():
-            @pl.when(core == 0)
-            def _():
-                halo_down(1).wait_recv()
-
-            @pl.when(core == 1)
-            def _():
-                halo_up(1).wait_recv()
-
-        @pl.when(jnp.logical_and(has_prev, n == 5))
-        def _():
-            @pl.when(core == 0)
-            def _():
-                halo_up(1).wait_recv()
-
-            @pl.when(core == 1)
-            def _():
-                halo_down(1).wait_recv()
-
-        @pl.when(jnp.logical_not(jnp.logical_and(n == 4, at_rim)))
-        def _():
-            add_row(far, which, n, 0)
-
-        return carry
-
-    lax.fori_loop(0, 6, far_step, 0)
-    even = base[:, :outs]
-    odd = base[:, outs:]
+        add_row(far, which, n, 0)
+
+        @pl.when(n == 1)
+        def _():
+            for dx in range(3):
+                z = shifted(near[dx], dx)
+                base[:, :outs] += z[:, outs:]
+                base[:, outs:] += z[:, :outs] + z[:, outs:]
+
+        return carry
+
+    lax.fori_loop(0, 4, far_step, 0)
     for dx in range(3):
         z = shifted(far[dx], dx)
-        even = even + (z[:, :outs] + z[:, outs:])
-        odd = odd + z[:, :outs]
-    out_ref[0] = even.astype(BF16)
-    out_ref[1] = odd.astype(BF16)
+        base[:, :outs] += z[:, :outs] + z[:, outs:]
+        base[:, outs:] += z[:, :outs]
+
+    place = lax.broadcasted_iota(jnp.int32, (cols, 1), 0)
+
+    def last_step(n, carry):
+        from_above = jnp.where(n == 4, core == 0, core == 1)
+
+        @pl.when(jnp.logical_and(has_prev, from_above))
+        def _():
+            halo_down(1).wait_recv()
+
+        @pl.when(jnp.logical_and(has_prev, jnp.logical_not(from_above)))
+        def _():
+            halo_up(1).wait_recv()
+
+        source, target, dy = visit(n)
+        row = act[which, source]
+        row = jnp.where(jnp.logical_and(n == 4, at_rim), jnp.zeros_like(row), row)
+        part = pl.ds(pl.multiple_of(target * cols, cols), cols)
+        even = base[part, :outs]
+        odd = base[part, outs:]
+        for dx in range(3):
+            z = jnp.dot(row, wc[dx, dy, :, :2 * outs], preferred_element_type=F32)
+            if dx == 0:
+                z = jnp.where(place == 0, 0.0, pltpu.roll(z, 1, 0))
+            if dx == 2:
+                z = jnp.where(place == cols - 1, 0.0, pltpu.roll(z, cols - 1, 0))
+            even = even + (z[:, :outs] + z[:, outs:])
+            odd = odd + z[:, :outs]
+        out_ref[0, part, :] = even.astype(BF16)
+        out_ref[1, part, :] = odd.astype(BF16)
+        return carry
+
+    lax.fori_loop(4, 6, last_step, 0)
 
     for h in range(2):
         for lane in range(2):
@@ -452,6 +478,7 @@
             pltpu.VMEM((channels, channels), BF16),
             pltpu.VMEM((channels, channels), BF16),
             pltpu.VMEM((channels, channels), BF16),
+            pltpu.VMEM((channels, channels), BF16),
             pltpu.VMEM((channels, outs), BF16),
             pltpu.VMEM((2, 4, cols, channels), BF16),
             pltpu.VMEM((cells, channels), BF16),

time: 52.1 us -> 51.4 us (0.987)
  the two profiles are of different devices: /device:TPU:321 before, /device:TPU:384 now
where the time goes in v4:
time: 51.4 us; the launch traced here: 51.3 us
  Pallas kernels  50.5 us (98%)
  local copies, waits for them, and re-layouts  0.73 us (1%)
    pallas_call x1, Pallas kernels, per_device(): pl.pallas_call(functools.partial(kernel, spans, tiles), out_shape=jax.Sha...  50.5 us

profile of v4, /device:TPU:384, one launch (start us, length us, event | category | flops | bytes accessed | tf_op | source)
XLA Modules:
  0.0 51.3 jit_solution(13972617292321067941)
XLA Ops:
  0.0 50.5 %mid_block_decode.1 = bf16[2,320,256]{2,1,0:T(8,128)(2,1)S(1)} custom-call(bf16[2,160,512]{2,1,0:T(8,128)(2,1)} %bitcast.4, f32[1,512]{1,0:T(1,128)} %bitcast.5, bf16[512,512]{1,0:T(8,128)(2,1)} %wq_hbm.1, bf16[512,512]{1,0:T(8,128)(2,1)} %wk_hbm.1, bf16[512,512]{1,0:T(8,128)(2,1)} %wv_hbm.1, bf16[512,512]{1,0:T(8,128)(2,1)} %wo_hbm.1, ...), custom_call_target="tpu_custom_call" | custom-call | tf_op jit(solution)/shard_map/mid_block_decode/pallas_call | solution.py:463
  50.5 0.7 %copy.10 = bf16[2,2,160,256]{3,2,1,0:T(8,128)(2,1)} copy(bf16[2,2,160,256]{3,2,1,0:T(8,128)(2,1)S(1)} %bitcast.3) | data formatting | bytes 655360

commit v5 on v4

--- a/solution.py
+++ b/solution.py
@@ -73,18 +73,16 @@
 
     barrier = pltpu.get_barrier_semaphore()
 
-    def greet(k, carry):
-        pl.semaphore_signal(barrier, inc=1, device_id=(t, lax.rem(i + k, tiles)), device_id_type=MESH)
-        return carry
-
-    lax.fori_loop(1, tiles, greet, 0)
+    edge_peer = jnp.where(core == 0, above, below)
+    for peer in (right, left, sibling, edge_peer):
+        pl.semaphore_signal(barrier, inc=1, device_id=(t, peer), device_id_type=MESH)
 
     @pl.when(has_prev)
     def _():
         pl.semaphore_signal(barrier, inc=1, device_id=(t_prev, i), device_id_type=MESH)
 
     loads[0].wait()
-    pl.semaphore_wait(barrier, tiles - 1 + jnp.where(has_next, 1, 0))
+    pl.semaphore_wait(barrier, 4 + jnp.where(has_next, 1, 0))
 
     def first(h, lane):
         row = h if lane == 0 else 1 - h
@@ -113,16 +111,32 @@
         packed = jnp.where(lane_of == k, source[:, b * 128:(b + 1) * 128], packed)
     stats[0] = packed[0:1]
 
-    def stat_copy(k):
-        return remote(
-            stats.at[0], stats.at[k], st_send.at[k], st_recv.at[k], (t, lax.rem(i + k, tiles))
-        )
-
-    def send_stat(k, carry):
-        stat_copy(k).start()
-        return carry
-
-    lax.fori_loop(1, tiles, send_stat, 0)
+    half = steps // 2
+
+    def sums_right(d):
+        return remote(
+            stats.at[d - 1], stats.at[d], st_send.at[d], st_recv.at[d], (t, right)
+        )
+
+    def sums_left(d):
+        source = jnp.where(d == 1, 0, half + d - 1)
+        return remote(
+            stats.at[source], stats.at[half + d], st_send.at[half + d], st_recv.at[half + d], (t, left)
+        )
+
+    sums_across = remote(stats.at[steps], stats.at[steps + 1], st_send.at[steps], st_recv.at[steps], (t, sibling))
+
+    def relay(d):
+        sums_right(d).wait_recv()
+        sums_right(d + 1).start()
+        sums_left(d).wait_recv()
+
+        @pl.when(d < half - 1)
+        def _():
+            sums_left(d + 1).start()
+
+    sums_right(1).start()
+    sums_left(1).start()
     for lane in range(2):
         first(1, lane).start()
     for copy in loads[1:]:
@@ -146,14 +160,14 @@
         )
 
     def prepare():
-        def take(k, carry):
-            stat_copy(k).wait_recv()
-            return carry
-
-        lax.fori_loop(1, tiles, take, 0)
+        sums_right(half).wait_recv()
         whole = stats[0]
-        for k in range(1, tiles):
+        for k in range(1, steps):
             whole = whole + stats[k]
+        stats[steps] = whole
+        sums_across.start()
+        sums_across.wait_recv()
+        whole = whole + stats[steps + 1]
         whole = jnp.broadcast_to(whole, (8, 128))
         spread = [group_sum(jnp.where(lane_of == k, whole, 0.0), width) for k in range(2 * blocks)]
         population = float(tiles * cells * width)
@@ -233,29 +247,31 @@
         return carry
 
     def gather_step(e, carry):
+        @pl.when(e < half)
+        def _():
+            relay(e)
+
         arrive(e)
 
         @pl.when(e == 2)
-        def _():
-            prepare()
-
-        @pl.when(e == 3)
         def _():
             lax.fori_loop(0, 27, load_tap, 0)
             loads[4].wait()
             loads[5].wait()
             wvo[...] = jnp.dot(wv[...], wo[...], preferred_element_type=F32).astype(BF16)
 
-        low = jnp.where(e == 3, 1, e - 1)
-        low = jnp.where(e == 2, 0, low)
-        high = jnp.where(e == 2, 1, e)
-        high = jnp.where(e == steps - 2, steps - 1, high)
-        high = jnp.where(e == 1, low, high)
-        low = jnp.where(e == steps - 1, high, low)
+        @pl.when(e == half)
+        def _():
+            prepare()
+
+        low = jnp.where(e <= half, 0, 3 * (e - half - 1))
+        high = jnp.where(e <= half, 0, low + 3)
+        high = jnp.where(e == steps - 1, low, high)
         lax.fori_loop(low, high, attend_step, 0)
         return carry
 
     lax.fori_loop(1, steps, gather_step, 0)
+    attend_step(steps - 2, 0)
     attend(steps - 1, 0, 2)
     sib_copy(steps - 1).wait_recv()
     attend(steps - 1, 2, 2)
@@ -274,6 +290,9 @@
         return remote(
             act.at[0, 1 + row], act.at[1, 1 + row], edge_send.at[4 + row], edge_recv.at[4 + row], (t_next, i)
         )
+
+    across = remote(act.at[0, 0], act.at[1, 0], edge_send.at[6], edge_recv.at[6], (t_next, i))
+    back = remote(act.at[1, 0], act.at[1, 2], edge_send.at[7], edge_recv.at[7], (t, above))
 
     def send_halo(which, row):
         @pl.when(row == 0)
@@ -294,14 +313,24 @@
         wide = mid_row.astype(F32)
         act[0, 1 + row] = (wide * (1.0 / (1.0 + jnp.exp(-wide)))).astype(BF16)
 
+        @pl.when(jnp.logical_and(has_next, k == 0))
+        def _():
+            onward(row).start()
+
+        send_halo(0, row)
+        return carry
+
+    lax.fori_loop(0, 2, finish, 0)
+
+    @pl.when(core == 1)
+    def _():
+        halo_down(0).wait_recv()
+
         @pl.when(has_next)
         def _():
-            onward(row).start()
-
-        send_halo(0, row)
-        return carry
-
-    lax.fori_loop(0, 2, finish, 0)
+            across.start()
+            onward(0).start()
+
 
     loads[6].wait()
     skip = jnp.dot(mid[...], ws[...], preferred_element_type=F32)
@@ -344,7 +373,11 @@
         @pl.when(n == 4)
         def _():
             halo_up(0).wait_recv()
-            halo_down(0).wait_recv()
+
+            @pl.when(core == 0)
+            def _():
+                halo_down(0).wait_recv()
+
 
         @pl.when(jnp.logical_not(jnp.logical_and(n == 4, at_rim)))
         def _():
@@ -356,11 +389,23 @@
     which = jnp.where(t == 0, 0, 1)
 
     def far_step(n, carry):
-        @pl.when(jnp.logical_and(has_prev, lax.rem(n, 2) == 0))
-        def _():
-            row = jnp.where(n == 0, core, 1 - core)
-            onward(row).wait_recv()
-            send_halo(1, row)
+        @pl.when(jnp.logical_and(has_prev, n == 0))
+        def _():
+            onward(core).wait_recv()
+            send_halo(1, core)
+
+        @pl.when(jnp.logical_and(has_prev, n == 2))
+        def _():
+            @pl.when(core == 0)
+            def _():
+                back.wait_recv()
+
+            @pl.when(core == 1)
+            def _():
+                across.wait_recv()
+                back.start()
+                onward(0).wait_recv()
+                halo_up(1).start()
 
         add_row(far, which, n, 0)
 
@@ -381,14 +426,14 @@
 
     place = lax.broadcasted_iota(jnp.int32, (cols, 1), 0)
 
-    def last_step(n, carry):
-        from_above = jnp.where(n == 4, core == 0, core == 1)
-
-        @pl.when(jnp.logical_and(has_prev, from_above))
+    def last_step(k, carry):
+        n = jnp.where(core == 0, k, 9 - k)
+
+        @pl.when(jnp.logical_and(has_prev, jnp.logical_and(core == 0, k == 4)))
         def _():
             halo_down(1).wait_recv()
 
-        @pl.when(jnp.logical_and(has_prev, jnp.logical_not(from_above)))
+        @pl.when(jnp.logical_and(has_prev, k == 5))
         def _():
             halo_up(1).wait_recv()
 
@@ -427,23 +472,31 @@
 
     lax.fori_loop(1, steps, drain, 0)
 
-    def drain_stat(k, carry):
-        stat_copy(k).wait_send()
-        return carry
-
-    lax.fori_loop(1, tiles, drain_stat, 0)
+    for d in range(1, half + 1):
+        sums_right(d).wait_send()
+    for d in range(1, half):
+        sums_left(d).wait_send()
+    sums_across.wait_send()
     halo_up(0).wait_send()
     halo_down(0).wait_send()
 
     @pl.when(has_prev)
     def _():
         halo_up(1).wait_send()
-        halo_down(1).wait_send()
+
+        @pl.when(core == 1)
+        def _():
+            halo_down(1).wait_send()
+            back.wait_send()
 
     @pl.when(has_next)
     def _():
-        for row in range(2):
-            onward(row).wait_send()
+        onward(0).wait_send()
+
+        @pl.when(core == 1)
+        def _():
+            onward(1).wait_send()
+            across.wait_send()
 
 
 def per_device(
@@ -471,7 +524,7 @@
             pltpu.VMEM((cells, channels), F32),
             pltpu.VMEM((cells, 128), F32),
             pltpu.VMEM((cells, 128), F32),
-            pltpu.VMEM((tiles, 1, 128), F32),
+            pltpu.VMEM((steps + 2, 1, 128), F32),
             pltpu.VMEM((8, channels), F32),
             pltpu.VMEM((1, channels), F32),
             pltpu.VMEM((channels, channels), BF16),
@@ -486,8 +539,8 @@
             pltpu.VMEM((3, cells, 2 * outs), F32),
             pltpu.VMEM((cells, 2 * outs), F32),
             pltpu.VMEM((3, 3, channels, 3 * outs), BF16),
-            dma((steps, 2)), dma((steps, 2)), dma((steps,)), dma((steps,)), dma((tiles,)), dma((tiles,)), dma((7,)),
-            dma((6,)), dma((6,)), dma((27,)),
+            dma((steps, 2)), dma((steps, 2)), dma((steps,)), dma((steps,)), dma((steps + 1,)), dma((steps + 1,)), dma((7,)),
+            dma((8,)), dma((8,)), dma((27,)),
         ],
         compiler_params=pltpu.CompilerParams(
             collective_id=0, has_side_effects=True, vmem_limit_bytes=50 * 1024 * 1024

time: 51.4 us -> 50.7 us (0.986)
  the two profiles are of different devices: /device:TPU:384 before, /device:TPU:1 now
where the time goes in v5:
time: 50.7 us; the launch traced here: 49.9 us
  Pallas kernels  49.1 us (97%)
  local copies, waits for them, and re-layouts  0.73 us (1%)
    pallas_call x1, Pallas kernels, per_device(): pl.pallas_call(functools.partial(kernel, spans, tiles), out_shape=jax.Sha...  49.1 us

profile of v5, /device:TPU:1, one launch (start us, length us, event | category | flops | bytes accessed | tf_op | source)
XLA Modules:
  0.0 49.9 jit_solution(8655419788776733625)
XLA Ops:
  0.0 49.1 %mid_block_decode.1 = bf16[2,320,256]{2,1,0:T(8,128)(2,1)S(1)} custom-call(bf16[2,160,512]{2,1,0:T(8,128)(2,1)} %bitcast.4, f32[1,512]{1,0:T(1,128)} %bitcast.5, bf16[512,512]{1,0:T(8,128)(2,1)} %wq_hbm.1, bf16[512,512]{1,0:T(8,128)(2,1)} %wk_hbm.1, bf16[512,512]{1,0:T(8,128)(2,1)} %wv_hbm.1, bf16[512,512]{1,0:T(8,128)(2,1)} %wo_hbm.1, ...), custom_call_target="tpu_custom_call" | custom-call | tf_op jit(solution)/shard_map/mid_block_decode/pallas_call | solution.py:516
  49.1 0.7 %copy.10 = bf16[2,2,160,256]{3,2,1,0:T(8,128)(2,1)} copy(bf16[2,2,160,256]{3,2,1,0:T(8,128)(2,1)S(1)} %bitcast.3) | data formatting | bytes 655360

commit v6 on v5

--- a/solution.py
+++ b/solution.py
@@ -109,7 +109,7 @@
         source = sums if k < blocks else squares
         b = k % blocks
         packed = jnp.where(lane_of == k, source[:, b * 128:(b + 1) * 128], packed)
-    stats[0] = packed[0:1]
+    stats[tiles // 2] = packed[0:1]
 
     half = steps // 2
 
@@ -135,6 +135,9 @@
         def _():
             sums_left(d + 1).start()
 
+    sums_across.start()
+    sums_across.wait_recv()
+    stats[0] = stats[steps] + stats[steps + 1]
     sums_right(1).start()
     sums_left(1).start()
     for lane in range(2):
@@ -164,10 +167,6 @@
         whole = stats[0]
         for k in range(1, steps):
             whole = whole + stats[k]
-        stats[steps] = whole
-        sums_across.start()
-        sums_across.wait_recv()
-        whole = whole + stats[steps + 1]
         whole = jnp.broadcast_to(whole, (8, 128))
         spread = [group_sum(jnp.where(lane_of == k, whole, 0.0), width) for k in range(2 * blocks)]
         population = float(tiles * cells * width)
@@ -190,16 +189,18 @@
         total[...] = jnp.zeros_like(total)
         peak[...] = jnp.full_like(peak, -jnp.inf)
 
-    def attend(e, begin, count):
+    everything = pl.ds(0, cells)
+
+    def attend(e, begin, count, part=everything):
         keys = slots[e, begin:begin + count].reshape(count * cols, channels)
-        scores = lax.dot_general(q2[...], keys, (((1,), (1,)), ((), ())), preferred_element_type=F32)
-        before = peak[:, 0:1]
+        scores = lax.dot_general(q2[part, :], keys, (((1,), (1,)), ((), ())), preferred_element_type=F32)
+        before = peak[part, 0:1]
         now = jnp.maximum(before, jnp.max(scores, axis=1, keepdims=True))
         fade = jnp.exp2(before - now)
         weights = jnp.exp2(scores - now).astype(BF16)
-        peak[...] = jnp.broadcast_to(now, peak.shape)
-        total[...] = total[...] * fade + jnp.sum(weights.astype(F32), axis=1, keepdims=True)
-        acc[...] = acc[...] * fade + jnp.dot(weights, keys, preferred_element_type=F32)
+        peak[part, :] = jnp.broadcast_to(now, (now.shape[0], 128))
+        total[part, :] = total[part, :] * fade + jnp.sum(weights.astype(F32), axis=1, keepdims=True)
+        acc[part, :] = acc[part, :] * fade + jnp.dot(weights, keys, preferred_element_type=F32)
 
     def arrive(e):
         for lane in range(2):
@@ -264,8 +265,9 @@
         def _():
             prepare()
 
-        low = jnp.where(e <= half, 0, 3 * (e - half - 1))
-        high = jnp.where(e <= half, 0, low + 3)
+        low = jnp.where(e <= half, 0, jnp.where(e == half + 1, 1, half))
+        high = jnp.where(e <= half, 1, jnp.where(e == half + 1, half, steps - 2))
+        high = jnp.where(e < half, 0, high)
         high = jnp.where(e == steps - 1, low, high)
         lax.fori_loop(low, high, attend_step, 0)
         return carry
@@ -274,7 +276,6 @@
     attend_step(steps - 2, 0)
     attend(steps - 1, 0, 2)
     sib_copy(steps - 1).wait_recv()
-    attend(steps - 1, 2, 2)
 
     def halo_up(which):
         return remote(
@@ -306,6 +307,7 @@
     def finish(k, carry):
         row = k + core - 2 * k * core
         part = pl.ds(pl.multiple_of(row * cols, cols), cols)
+        attend(steps - 1, 2, 2, part)
         mixed = (acc[part, :] * (1.0 / total[part, 0:1]) * ab[0:1] + ab[1:2]).astype(BF16)
         change = jnp.dot(mixed, wvo[...], preferred_element_type=F32)
         mid_row = (slots[0, row].astype(F32) + change).astype(BF16)

time: 50.7 us -> 50.2 us (level); the launches traced: 49.9 us -> 50 us
  no operation moved by 1% of the time
where the time goes in v6:
time: 50.2 us; the launch traced here: 50 us
  Pallas kernels  49.2 us (98%)
  local copies, waits for them, and re-layouts  0.73 us (1%)
    pallas_call x1, Pallas kernels, per_device(): pl.pallas_call(functools.partial(kernel, spans, tiles), out_shape=jax.Sha...  49.2 us

profile of v6, /device:TPU:1, one launch (start us, length us, event | category | flops | bytes accessed | tf_op | source)
XLA Modules:
  0.0 50.0 jit_solution(6496760511323073229)
XLA Ops:
  0.0 49.2 %mid_block_decode.1 = bf16[2,320,256]{2,1,0:T(8,128)(2,1)S(1)} custom-call(bf16[2,160,512]{2,1,0:T(8,128)(2,1)} %bitcast.4, f32[1,512]{1,0:T(1,128)} %bitcast.5, bf16[512,512]{1,0:T(8,128)(2,1)} %wq_hbm.1, bf16[512,512]{1,0:T(8,128)(2,1)} %wk_hbm.1, bf16[512,512]{1,0:T(8,128)(2,1)} %wv_hbm.1, bf16[512,512]{1,0:T(8,128)(2,1)} %wo_hbm.1, ...), custom_call_target="tpu_custom_call" | custom-call | tf_op jit(solution)/shard_map/mid_block_decode/pallas_call | solution.py:518
  49.2 0.7 %copy.10 = bf16[2,2,160,256]{3,2,1,0:T(8,128)(2,1)} copy(bf16[2,2,160,256]{3,2,1,0:T(8,128)(2,1)S(1)} %bitcast.3) | data formatting | bytes 655360

commit v7 on v6

--- a/solution.py
+++ b/solution.py
@@ -396,16 +396,23 @@
             onward(core).wait_recv()
             send_halo(1, core)
 
-        @pl.when(jnp.logical_and(has_prev, n == 2))
-        def _():
-            @pl.when(core == 0)
+        @pl.when(jnp.logical_and(n == 2, core == 0))
+        def _():
+            @pl.when(has_prev)
             def _():
                 back.wait_recv()
 
-            @pl.when(core == 1)
+        @pl.when(jnp.logical_and(n == 2, core == 1))
+        def _():
+            @pl.when(has_prev)
             def _():
                 across.wait_recv()
                 back.start()
+
+            add_row(far, which, 5, 0)
+
+            @pl.when(has_prev)
+            def _():
                 onward(0).wait_recv()
                 halo_up(1).start()
 
@@ -428,8 +435,13 @@
 
     place = lax.broadcasted_iota(jnp.int32, (cols, 1), 0)
 
+    @pl.when(core == 1)
+    def _():
+        out_ref[0, 0:cols, :] = base[0:cols, :outs].astype(BF16)
+        out_ref[1, 0:cols, :] = base[0:cols, outs:].astype(BF16)
+
     def last_step(k, carry):
-        n = jnp.where(core == 0, k, 9 - k)
+        n = jnp.where(core == 0, k, 4)
 
         @pl.when(jnp.logical_and(has_prev, jnp.logical_and(core == 0, k == 4)))
         def _():
@@ -457,7 +469,7 @@
         out_ref[1, part, :] = odd.astype(BF16)
         return carry
 
-    lax.fori_loop(4, 6, last_step, 0)
+    lax.fori_loop(4 + core, 6, last_step, 0)
 
     for h in range(2):
         for lane in range(2):

time: 50.2 us -> 50.1 us (level)
  no operation moved by 1% of the time
where the time goes in v7:
time: 50.1 us; the launch traced here: 49.9 us
  Pallas kernels  49.2 us (98%)
  local copies, waits for them, and re-layouts  0.73 us (1%)
    pallas_call x1, Pallas kernels, per_device(): pl.pallas_call(functools.partial(kernel, spans, tiles), out_shape=jax.Sha...  49.2 us

profile of v7, /device:TPU:1, one launch (start us, length us, event | category | flops | bytes accessed | tf_op | source)
XLA Modules:
  0.0 49.9 jit_solution(4030513912091655462)
XLA Ops:
  0.0 49.2 %mid_block_decode.1 = bf16[2,320,256]{2,1,0:T(8,128)(2,1)S(1)} custom-call(bf16[2,160,512]{2,1,0:T(8,128)(2,1)} %bitcast.4, f32[1,512]{1,0:T(1,128)} %bitcast.5, bf16[512,512]{1,0:T(8,128)(2,1)} %wq_hbm.1, bf16[512,512]{1,0:T(8,128)(2,1)} %wk_hbm.1, bf16[512,512]{1,0:T(8,128)(2,1)} %wv_hbm.1, bf16[512,512]{1,0:T(8,128)(2,1)} %wo_hbm.1, ...), custom_call_target="tpu_custom_call" | custom-call | tf_op jit(solution)/shard_map/mid_block_decode/pallas_call | solution.py:530
  49.2 0.7 %copy.10 = bf16[2,2,160,256]{3,2,1,0:T(8,128)(2,1)} copy(bf16[2,2,160,256]{3,2,1,0:T(8,128)(2,1)S(1)} %bitcast.3) | data formatting | bytes 655360
